TPU v7x, 128 devices: a whole 4x4x4 slice. The times are simulated.
128 devices in a mesh: row: 8 (over x, core), col: 16 (over y, z).
Axes of the slice: x: 4, y: 4, z: 4, core: 2. Of those that a mesh axis runs over, the one named last changes fastest.
Arguments:
- front_blocks: float32 [16, 1024, 8, 2048], P(None, 'row', None, 'col'), may hold values from -2.5 to 10.5, as said below
- child_updates: bfloat16 [2, 12, 1024, 6, 2048], P(None, None, 'row', None, 'col'), may hold values from -0.2 to 2.2, as said below
- child_map: int32 [2, 96], replicated, may hold values from 0 to 127, as said below
Outputs:
- factored: float32 [16, 1024, 8, 2048], P(None, 'row', None, 'col')
Inputs may be any that keep to these rules, and one draw needn't show every extreme that they name: `child_map`: for each child, block a * 16 + j (0 <= j < 16) lands in front block h_a * 16 + ((s_a - j) mod 16), with 6 distinct h_a below 8 and s_a = (s + q_a) mod 16, q a permutation of 0 .. 5. Hence along col one device sends at most 1 of a child's column blocks to one device, along row at most 2 of its row blocks, and both bounds are reached in every draw. `front_blocks`: symmetric positive definite. `child_updates`: each child update is symmetric.
All inputs are finite; a program needn't handle non-finite values.
Results may differ from a plain program's by a relative error of at most 0.0003.
Values may be sent and summed in bfloat16 or wider, within the bound.
A program may use at most 192 MiB of HBM per device.

v0:
```python
import jax
import jax.numpy as jnp
from jax import lax
from jax.sharding import PartitionSpec as P

PW = 256
PANELS = 2
PD = 512


def spread_2(value, axis, source):
    kept = jnp.where(lax.axis_index(axis) == source, value, 0).astype(value.dtype)
    return lax.psum(kept, axis)


def earlier_count(targets):
    count_all = targets.shape[1]
    matches = targets[:, :, None, :] == targets[:, None, :, :]
    order_ids = jnp.arange(count_all)
    before = (order_ids[None, :] < order_ids[:, None])[None, :, :, None]
    return jnp.sum(matches & before, axis=2)


def arrival_info(block_map, my_index, devices):
    child_count = block_map.shape[0]
    slot_total = block_map.shape[1] // devices
    block_grid = block_map.reshape(child_count, slot_total, devices)
    targets = block_grid % devices
    home_slots = block_grid // devices
    arriving = targets == my_index
    arrival_flat = arriving.reshape(child_count, slot_total * devices).astype(jnp.int32)
    positions = (jnp.cumsum(arrival_flat, axis=1) - 1).reshape(child_count, slot_total, devices)
    return (targets, home_slots, arriving, positions)


def route_tables(block_map, my_index, devices, capacity, slot_count):
    child_count = block_map.shape[0]
    slot_total = block_map.shape[1] // devices
    targets, home_slots, arriving, positions = arrival_info(block_map, my_index, devices)
    slot_ranks = earlier_count(targets)
    my_targets = lax.dynamic_index_in_dim(targets, my_index, axis=2, keepdims=False)
    my_ranks = lax.dynamic_index_in_dim(slot_ranks, my_index, axis=2, keepdims=False)
    child_ids = jnp.arange(child_count)[:, None]
    slot_values = jnp.broadcast_to(
        jnp.arange(slot_total, dtype=jnp.int32)[None, :], (child_count, slot_total)
    )
    send_index = jnp.full((child_count, devices * capacity), slot_total, jnp.int32)
    send_index = send_index.at[child_ids, my_targets * capacity + my_ranks].set(slot_values)
    sources = jnp.arange(devices, dtype=jnp.int32)[None, None, :]
    where_from = jnp.where(arriving, sources * capacity + slot_ranks, devices * capacity)
    where_to = jnp.where(arriving, home_slots, slot_count)
    place_index = jnp.full((child_count, slot_count + 1), devices * capacity, jnp.int32)
    place_index = place_index.at[child_ids[:, :, None], where_to].set(where_from)
    return (send_index, place_index[:, :slot_count])


def pick_slots(payload, index_table, axis_no):
    return jax.vmap(lambda part_data, part_index: jnp.take(part_data, part_index, axis=axis_no))(
        payload, index_table
    )


def move_rows(payload, block_map, slot_count):
    devices = lax.axis_size("row")
    my_index = lax.axis_index("row")
    col_devices = lax.axis_size("col")
    child_count, slot_total, tile_size, row_width = payload.shape
    col_slots = block_map.shape[1] // col_devices
    capacity = col_devices // devices * ((col_slots + devices - 1) // devices)
    send_index, place_index = route_tables(block_map, my_index, devices, capacity, slot_count)
    padded = jnp.concatenate(
        [payload, jnp.zeros((child_count, 1, tile_size, row_width), payload.dtype)], axis=1
    )
    outgoing = pick_slots(padded, send_index, 0).reshape(
        child_count, devices * capacity * tile_size, row_width
    )
    incoming = lax.all_to_all(outgoing, "row", split_axis=1, concat_axis=1, tiled=True)
    incoming = incoming.reshape(child_count, devices * capacity, tile_size, row_width)
    padded_in = jnp.concatenate(
        [incoming, jnp.zeros((child_count, 1, tile_size, row_width), incoming.dtype)], axis=1
    )
    return pick_slots(padded_in, place_index, 0)


def move_columns(payload, block_map, slot_count):
    devices = lax.axis_size("col")
    my_index = lax.axis_index("col")
    child_count, height, slot_total, tile_size = payload.shape
    capacity = (slot_total + devices - 1) // devices
    send_index, place_index = route_tables(block_map, my_index, devices, capacity, slot_count)
    padded = jnp.concatenate(
        [payload, jnp.zeros((child_count, height, 1, tile_size), payload.dtype)], axis=2
    )
    outgoing = pick_slots(padded, send_index, 1).reshape(
        child_count, height, devices * capacity * tile_size
    )
    incoming = lax.all_to_all(outgoing, "col", split_axis=2, concat_axis=2, tiled=True)
    incoming = incoming.reshape(child_count, height, devices * capacity, tile_size)
    padded_in = jnp.concatenate(
        [incoming, jnp.zeros((child_count, height, 1, tile_size), incoming.dtype)], axis=2
    )
    return pick_slots(padded_in, place_index, 1)


def on_device(front_blocks, child_updates, child_map):
    row_count = lax.axis_size("row")
    col_count = lax.axis_size("col")
    row_index = lax.axis_index("row")
    col_index = lax.axis_index("col")
    front_slots_r = front_blocks.shape[0]
    tile_size = front_blocks.shape[1]
    front_slots_c = front_blocks.shape[2]
    child_count = child_updates.shape[0]
    child_rows = child_updates.shape[1]
    child_cols = child_updates.shape[3]
    arrived = move_rows(
        child_updates.reshape(child_count, child_rows, tile_size, child_cols * tile_size),
        child_map,
        front_slots_r,
    )
    arrived = move_columns(
        arrived.reshape(child_count, front_slots_r * tile_size, child_cols, tile_size),
        child_map,
        front_slots_c,
    )
    height = front_slots_r * tile_size
    breadth = front_slots_c * tile_size
    children_sum = jnp.sum(arrived.astype(jnp.float32), axis=0).reshape(height, breadth)
    assembled = front_blocks.reshape(height, breadth) + children_sum
    local_rows = jnp.arange(height, dtype=jnp.int32)
    row_global = (
        local_rows // tile_size * row_count + row_index
    ) * tile_size + local_rows % tile_size
    local_cols = jnp.arange(breadth, dtype=jnp.int32)
    col_global = (
        local_cols // tile_size * col_count + col_index
    ) * tile_size + local_cols % tile_size
    panel_tiles = PW // tile_size
    spread = col_count // row_count
    row_factors = []
    col_factors = []
    for panel_no in range(PANELS):
        first_col = panel_no * PW
        finish = first_col + PW
        column_tiles = []
        for tile_no in range(panel_tiles):
            global_tile = panel_no * panel_tiles + tile_no
            col_slot = global_tile // col_count
            column_tile = assembled[:, col_slot * tile_size : (col_slot + 1) * tile_size]
            column_tiles.append(column_tile)
        pieces = [
            jnp.where(
                col_index == (panel_no * panel_tiles + tile_no) % col_count,
                column_tiles[tile_no],
                0.0,
            )
            for tile_no in range(panel_tiles)
        ]
        panel_rows = lax.psum(jnp.concatenate(pieces, axis=1), "col")
        diag_pieces = []
        for tile_no in range(panel_tiles):
            global_tile = panel_no * panel_tiles + tile_no
            row_slot = global_tile // row_count
            diag_pieces.append(
                jnp.where(
                    row_index == global_tile % row_count,
                    panel_rows[row_slot * tile_size : (row_slot + 1) * tile_size],
                    0.0,
                )
            )
        diagonal = lax.psum(jnp.concatenate(diag_pieces, axis=0), "row")
        factor = jnp.linalg.cholesky(diagonal)
        solved = lax.linalg.triangular_solve(
            factor, panel_rows, left_side=False, lower=True, transpose_a=True
        )
        lower_part = jnp.where(row_global[:, None] >= finish, solved, 0.0)
        inside = (row_global >= first_col) & (row_global < finish)
        factor_rows = jnp.take(factor, jnp.clip(row_global - first_col, 0, PW - 1), axis=0)
        lower_part = jnp.where(inside[:, None], factor_rows, lower_part)
        chosen = lax.dynamic_index_in_dim(
            lower_part.reshape(front_slots_c, spread, tile_size, PW),
            col_index // row_count,
            axis=1,
            keepdims=False,
        ).reshape(breadth, PW)
        col_part = spread_2(chosen, "row", col_index % row_count)
        assembled = assembled - jnp.dot(
            lower_part,
            col_part.T,
            precision=lax.Precision.HIGHEST,
            preferred_element_type=jnp.float32,
        )
        row_factors.append(lower_part)
        col_factors.append(col_part)
    result = assembled
    for panel_no in range(PANELS):
        for tile_no in range(panel_tiles):
            global_tile = panel_no * panel_tiles + tile_no
            col_slot = global_tile // col_count
            owner_here = col_index == global_tile % col_count
            current = result[:, col_slot * tile_size : (col_slot + 1) * tile_size]
            fresh = row_factors[panel_no][:, tile_no * tile_size : (tile_no + 1) * tile_size]
            result = result.at[:, col_slot * tile_size : (col_slot + 1) * tile_size].set(
                jnp.where(owner_here, fresh, current)
            )
    upper_mask = (row_global[:, None] < PD) & (col_global[None, :] >= PD)
    result = jnp.where(upper_mask, 0.0, result)
    return result.reshape(front_slots_r, tile_size, front_slots_c, tile_size)


def solution(mesh):
    placed = (P(None, "row", None, "col"), P(None, None, "row", None, "col"), P())
    return jax.shard_map(
        on_device,
        mesh=mesh,
        in_specs=placed,
        out_specs=P(None, "row", None, "col"),
        check_vma=False,
    )
```

profile of v0, /device:TPU:1, one launch (start us, length us, event | category | flops | bytes accessed | tf_op | source)
XLA Modules:
  0.0 1364.7 jit_solution(4621265916315295728)
XLA Ops:
  10.4 2.0 scatter_fusion.3
  13.6 6.6 copy.72
  20.2 5.1 concatenate.51
  25.4 6.5 gather_fusion
  31.9 8.7 copy.73
  40.8 9.3 scatter_fusion.2
  50.2 4.1 bitcast_select_fusion.1
  54.3 44.7 %copy.74 = bf16[2,2048,768]{2,0,1:T(2,128)(2,1)} copy(bf16[2,2048,768]{2,1,0:T(8,128)(2,1)S(1)} %bitcast_select_fusion.1) | data formatting | bytes 12582912 | tf_op jit(solution)/shard_map/vmap(jit(_take))/select_n | solution.py:58
  99.0 6.3 all-to-all-start
  105.7 71.0 %all-to-all-done = bf16[2,2048,768]{2,0,1:T(2,128)(2,1)} async-done(((bf16[2,2048,768]{2,0,1:T(2,128)(2,1)}), bf16[2,2048,768]{2,0,1:T(2,128)(2,1)}, u32[]{:S(2)}, u32[]{:S(2)}) %all-to-all-start) | async-done | bytes 6291488 | tf_op jit(solution)/shard_map/all_to_all | solution.py:77
  176.6 3.6 copy.75
  180.2 3.8 concatenate.52
  184.0 6.5 gather_fusion.1
  190.6 13.6 reshape.731
  204.2 5.3 copy_select_fusion
  209.4 3.7 concatenate.53
  213.2 10.3 gather_fusion.2
  223.5 22.5 %copy.78 = bf16[2,2048,16,128]{1,3,2,0:T(8,128)(2,1)} copy(bf16[2,2048,16,128]{3,1,2,0:T(8,128)(2,1)} %bitcast.147) | data formatting | bytes 33554432 | tf_op jit(solution)/shard_map/vmap(jit(_take))/gather | solution.py:58
  246.0 8.5 bitcast_select_fusion
  254.5 48.9 %copy.79 = bf16[2,2048,2048]{1,0,2:T(2,128)(2,1)} copy(bf16[2,2048,2048]{1,2,0:T(8,128)(2,1)S(1)} %bitcast_select_fusion) | data formatting | bytes 33554432 | tf_op jit(solution)/shard_map/vmap(jit(_take))/select_n | solution.py:58
  303.3 8.0 all-to-all-start.1
  311.9 9.3 scatter_fusion
  321.4 8.9 copy.116
  330.2 9.2 copy.94
  339.4 263.2 %all-to-all-done.1 = bf16[2,2048,2048]{1,0,2:T(2,128)(2,1)} async-done(((bf16[2,2048,2048]{1,0,2:T(2,128)(2,1)}), bf16[2,2048,2048]{1,0,2:T(2,128)(2,1)}, u32[]{:S(2)}, u32[]{:S(2)}) %all-to-all-start.1) | async-done | bytes 16777248 | tf_op jit(solution)/shard_map/all_to_all | solution.py:97
  602.6 41.1 %copy.81 = bf16[2,2048,16,128]{3,1,2,0:T(8,128)(2,1)} copy(bf16[2,2048,16,128]{1,0,3,2:T(2,128)(2,1)} %bitcast.9) | data formatting | bytes 33554432 | tf_op jit(solution)/shard_map/reshape | solution.py:98
  643.7 15.5 %concatenate.54 = bf16[2,2048,17,128]{3,1,2,0:T(8,128)(2,1)} pad(bf16[2,2048,16,128]{3,1,2,0:T(8,128)(2,1)} %copy.81, bf16[]{:T(256)} %constant.419.clone.1), padding=0_0x0_0x0_1x0_0 | pad | bytes 34603008 | tf_op jit(solution)/shard_map/concatenate | solution.py:99
  659.2 11.1 gather_fusion.3
  670.3 9.8 convert_reduce_fusion
  680.0 9.1 copy.82
  689.1 11.7 bitcast_add_fusion
  703.9 94.7 %all-reduce.12.cloned.1.call-done = f32[2048,256]{0,1:T(8,128)} async-done(((f32[2048,256]{0,1:T(8,128)}), f32[2048,256]{0,1:T(8,128)}) %all-reduce.12.cloned.1.call-update) | async-done | bytes 2097168 | tf_op jit(solution)/shard_map/psum | solution.py:159
  800.8 58.3 %all-reduce.14.cloned.1.call-done = f32[256,256]{0,1:T(8,128)} async-done(((f32[256,256]{0,1:T(8,128)}), f32[256,256]{0,1:T(8,128)}) %all-reduce.14.cloned.1.call-update) | async-done | bytes 262160 | tf_op jit(solution)/shard_map/psum | solution.py:171
  861.1 11.7 cholesky.130
  872.9 9.8 custom-call.29
  883.2 11.7 cholesky.147
  897.6 6.8 gather_fusion.4
  904.4 1.8 copy.84
  906.3 3.9 while.8
  910.2 19.7 %custom-call.30 = f32[2,128,128]{1,2,0:T(8,128)S(1)} custom-call(f32[2,128,128]{2,1,0:T(8,128)S(1)} %get-tuple-element.70), custom_call_target="InvertDiagBlocksLowerTriangular" | custom-call | tf_op jit(solution)/shard_map/triangular_solve/custom-call.0 | solution.py:173
  929.9 2.4 fusion.7
  932.3 2.3 convolution_subtract_fusion.3
  936.0 2.8 reshape.607
  938.8 4.8 fusion.3
  944.9 61.6 %all-reduce.16.cloned.1.call-done = f32[1024,256]{0,1:T(8,128)} async-done(((f32[1024,256]{0,1:T(8,128)}), f32[1024,256]{0,1:T(8,128)}) %all-reduce.16.cloned.1.call-update) | async-done | bytes 1048592 | tf_op jit(solution)/shard_map/psum | solution.py:13
  1006.5 10.8 convolution_subtract_fusion.1
  1017.3 3.4 copy-done
  1022.4 90.8 %all-reduce.18.cloned.1.call-done = f32[2048,256]{0,1:T(8,128)} async-done(((f32[2048,256]{0,1:T(8,128)}), f32[2048,256]{0,1:T(8,128)}) %all-reduce.18.cloned.1.call-update) | async-done | bytes 2097168 | tf_op jit(solution)/shard_map/psum | solution.py:159
  1115.0 58.5 %all-reduce.20.cloned.1.call-done = f32[256,256]{0,1:T(8,128)} async-done(((f32[256,256]{0,1:T(8,128)}), f32[256,256]{0,1:T(8,128)}) %all-reduce.20.cloned.1.call-update) | async-done | bytes 262160 | tf_op jit(solution)/shard_map/psum | solution.py:171
  1175.6 11.7 cholesky.164
  1187.4 9.8 custom-call.31
  1197.7 11.7 cholesky.181
  1212.0 8.8 gather_fusion.5
  1220.8 2.9 copy.87
  1223.7 3.9 while.9
  1227.6 19.7 %custom-call.32 = f32[2,128,128]{1,2,0:T(8,128)S(1)} custom-call(f32[2,128,128]{2,1,0:T(8,128)S(1)} %get-tuple-element.71), custom_call_target="InvertDiagBlocksLowerTriangular" | custom-call | tf_op jit(solution)/shard_map/triangular_solve/custom-call.0 | solution.py:173
  1247.3 2.4 fusion.5
  1249.7 2.3 convolution_subtract_fusion.2
  1254.8 4.0 reshape.608
  1258.8 4.8 fusion.4
  1265.5 61.0 %all-reduce.22.cloned.1.call-done = f32[1024,256]{0,1:T(8,128)} async-done(((f32[1024,256]{0,1:T(8,128)}), f32[1024,256]{0,1:T(8,128)}) %all-reduce.22.cloned.1.call-update) | async-done | bytes 1048592 | tf_op jit(solution)/shard_map/psum | solution.py:13
  1326.5 10.8 convolution_subtract_fusion
  1341.8 5.2 copy.105
  1347.0 10.7 copy.90
  (137 shorter events, 42.4 us)
Async XLA Ops:
  99.0 77.6 %all-to-all-start = ((bf16[2,2048,768]{2,0,1:T(2,128)(2,1)}), bf16[2,2048,768]{2,0,1:T(2,128)(2,1)}, u32[]{:S(2)}, u32[]{:S(2)}) async-start(bf16[2,2048,768]{2,0,1:T(2,128)(2,1)} %copy.74), calls=%async_computation | async-start | bytes 12582912 | tf_op jit(solution)/shard_map/all_to_all | solution.py:77
  303.3 8.3 copy-start.4
  303.3 299.3 %all-to-all-start.1 = ((bf16[2,2048,2048]{1,0,2:T(2,128)(2,1)}), bf16[2,2048,2048]{1,0,2:T(2,128)(2,1)}, u32[]{:S(2)}, u32[]{:S(2)}) async-start(bf16[2,2048,2048]{1,0,2:T(2,128)(2,1)} %copy.79), calls=%async_computation.1 | async-start | bytes 33554432 | tf_op jit(solution)/shard_map/all_to_all | solution.py:97
  311.4 487.2 %all-reduce.12.cloned.1.call-start = ((), (), s32[]{:S(2)}) async-start(), calls=%async_computation.2 | async-start | bytes 4194304 | tf_op jit(solution)/shard_map/psum | solution.py:159
  703.8 155.2 %all-reduce.14.cloned.1.call-start = ((), (), s32[]{:S(2)}) async-start(), calls=%async_computation.3 | async-start | bytes 524288 | tf_op jit(solution)/shard_map/psum | solution.py:171
  800.3 206.2 %all-reduce.16.cloned.1.call-start = ((), (), s32[]{:S(2)}) async-start(), calls=%async_computation.4 | async-start | bytes 2097152 | tf_op jit(solution)/shard_map/psum | solution.py:13
  929.8 5.8 copy-start.3
  944.8 168.4 %all-reduce.18.cloned.1.call-start = ((), (), s32[]{:S(2)}) async-start(), calls=%async_computation.5 | async-start | bytes 4194304 | tf_op jit(solution)/shard_map/psum | solution.py:159
  1017.3 3.4 copy-start
  1022.4 151.1 %all-reduce.20.cloned.1.call-start = ((), (), s32[]{:S(2)}) async-start(), calls=%async_computation.6 | async-start | bytes 524288 | tf_op jit(solution)/shard_map/psum | solution.py:171
  1114.9 211.5 %all-reduce.22.cloned.1.call-start = ((), (), s32[]{:S(2)}) async-start(), calls=%async_computation.7 | async-start | bytes 2097152 | tf_op jit(solution)/shard_map/psum | solution.py:13
  1247.3 5.8 copy-start.2
  1337.2 2.0 copy-start.1
Sparse Core Ops, SparseCore 0:
  704.0 94.6 all-reduce.11
  801.0 57.9 all-reduce.13
  944.9 61.4 all-reduce.15
  1022.5 90.6 all-reduce.17
  1115.5 57.9 all-reduce.19
  1264.9 61.4 all-reduce.21
where the time goes:
time: 1380 us; the launch traced here: 1360 us
  waiting for transfers between devices  759 us (55%)
  local copies, waits for them, and re-layouts  364 us (26%)
  other arithmetic  176 us (13%)
  matrix products  34.1 us (2%)
  between operations  16.9 us (1%)
  starting transfers between devices  15.2 us (1%)
    all_to_all x1, waiting for transfers between devices, move_columns(): lax.all_to_all(outgoing, 'col', split_axis=2, concat_axis=2, tiled=True)  263 us
    psum x2, waiting for transfers between devices, on_device(): panel_rows = lax.psum(jnp.concatenate(pieces, axis=1), 'col')  185 us
    psum x2, waiting for transfers between devices, spread_2(): return lax.psum(kept, axis)  123 us
    psum x2, waiting for transfers between devices, on_device(): diagonal = lax.psum(jnp.concatenate(diag_pieces, axis=0), 'row')  117 us
    select_n x2, local copies, waits for them, and re-layouts, pick_slots(): jnp.take(part_data, part_index, axis=axis_no)  93.5 us
    gather x11, local copies, waits for them, and re-layouts, pick_slots(): jnp.take(part_data, part_index, axis=axis_no)  79.5 us
    all_to_all x1, waiting for transfers between devices, move_rows(): lax.all_to_all(outgoing, 'row', split_axis=1, concat_axis=1, tiled=True)  71 us
    another operation x14, other arithmetic, on_device(): factor = jnp.linalg.cholesky(diagonal)  69.2 us
  transfers between devices with their start and end apart: 8, of which 8 were waited for; matrix products, arithmetic and copies ran while one was open for 2% of the time, Pallas kernels for 0%

commit v1 on v0

v1 whole, which is shorter than its diff:
```python
import jax
import jax.numpy as jnp
from jax import lax
from jax.sharding import PartitionSpec as P

PW = 256
PANELS = 2
PD = 512
HI = lax.Precision.HIGHEST


def decode_map(child_map, lanes):
    base = child_map[:, ::lanes]
    home = base // lanes
    shift = base % lanes
    groups = base.shape[1]
    prev = (shift - 1) % lanes
    has_prev = jnp.any(prev[:, :, None] == shift[:, None, :], axis=2)
    start = jnp.sum(jnp.where(has_prev, 0, shift), axis=1)
    order = (shift - start[:, None]) % lanes
    picks = order[:, :, None] == jnp.arange(groups)[None, None, :]
    inv = jnp.sum(jnp.where(picks, jnp.arange(groups)[None, :, None], 0), axis=1)
    return home, shift, start, inv


def routed(packets, axis, devices, start):
    groups = len(packets)

    def branch(sigma):
        def run(*pk):
            return tuple(
                lax.ppermute(
                    pk[q], axis, [(j, (sigma + q - j) % devices) for j in range(devices)]
                )
                for q in range(groups)
            )

        return run

    return lax.switch(start % devices, [branch(sg) for sg in range(devices)], *packets)


def spread_pieces(piece, axis, owners, devices, pieces_axis):
    parts = devices // owners
    size = piece.shape[pieces_axis] // parts
    me = lax.axis_index(axis)
    sub = lax.slice_in_dim(piece, 0, size, axis=pieces_axis)
    for m in range(1, parts):
        part = lax.slice_in_dim(piece, m * size, (m + 1) * size, axis=pieces_axis)
        got = lax.ppermute(part, axis, [(k, m * owners + k) for k in range(owners)])
        sub = jnp.where(me // owners == m, got, sub)
    return lax.all_gather(sub, axis, axis=0, tiled=False), parts, size


def on_device(front_blocks, child_updates, child_map, row_count, col_count):
    row_index = lax.axis_index("row")
    col_index = lax.axis_index("col")
    slots_r, tile, slots_c, _ = front_blocks.shape
    child_count, kr_count, _, kc_count, _ = child_updates.shape
    home, shift, start, inv = decode_map(child_map, col_count)
    groups = home.shape[1]

    dense = []
    for i in range(child_count):
        with jax.named_scope("child_route_cols"):
            x = child_updates[i].reshape(kr_count, tile, kc_count * tile)
            col_packets = [
                lax.dynamic_slice_in_dim(x, inv[i, q] * tile, tile, axis=2) for q in range(groups)
            ]
            got = routed(col_packets, "col", col_count, start[i])
            y = jnp.stack(got, axis=2)
        with jax.named_scope("child_route_rows"):
            row_packets = [
                lax.dynamic_slice_in_dim(y, inv[i, q] * 2, 2, axis=0) for q in range(groups)
            ]
            got = routed(row_packets, "row", row_count, start[i])
            z = jnp.stack(got, axis=0).reshape(groups * 2, tile, groups, tile)
        with jax.named_scope("child_place"):
            qs = jnp.arange(groups)
            a_of = inv[i]
            s_of = shift[i, a_of]
            h_of = home[i, a_of]
            src = (start[i] + qs - row_index) % row_count
            per_home = col_count // row_count
            first = ((s_of - src) % col_count) // row_count
            row_slot = jnp.stack(
                [per_home * h_of + first, per_home * h_of + 1 - first], axis=1
            ).reshape(-1)
            col_slot = h_of
            row_src = jnp.sum(
                jnp.where(
                    row_slot[None, :] == jnp.arange(slots_r)[:, None],
                    jnp.arange(groups * 2)[None, :] + 1,
                    0,
                ),
                axis=1,
            ) - 1
            row_src = jnp.where(row_src < 0, groups * 2, row_src)
            col_src = jnp.sum(
                jnp.where(
                    col_slot[None, :] == jnp.arange(slots_c)[:, None],
                    jnp.arange(groups)[None, :] + 1,
                    0,
                ),
                axis=1,
            ) - 1
            col_src = jnp.where(col_src < 0, groups, col_src)
            zp = jnp.concatenate([z, jnp.zeros((1, tile, groups, tile), z.dtype)], axis=0)
            zp = jnp.take(zp, row_src, axis=0)
            zp = jnp.concatenate([zp, jnp.zeros((slots_r, tile, 1, tile), z.dtype)], axis=2)
            dense.append(jnp.take(zp, col_src, axis=2))

    with jax.named_scope("assemble"):
        assembled = front_blocks
        for d in dense:
            assembled = assembled + d.astype(jnp.float32)
        height = slots_r * tile
        breadth = slots_c * tile
        a2 = assembled.reshape(height, breadth)

    local_rows = jnp.arange(height, dtype=jnp.int32)
    row_global = (local_rows // tile * row_count + row_index) * tile + local_rows % tile
    local_cols = jnp.arange(breadth, dtype=jnp.int32)
    col_global = (local_cols // tile * col_count + col_index) * tile + local_cols % tile
    owners = PD // tile

    with jax.named_scope("gather_panel_rows"):
        g, parts, size = spread_pieces(a2[:, 0:tile], "col", owners, col_count, 0)
        g = g.reshape(parts, owners, size, tile).transpose(0, 2, 1, 3)
        g_rows = g.reshape(height, PD)
    with jax.named_scope("gather_panel_cols"):
        g, parts, size = spread_pieces(a2[0:tile, :], "row", owners, row_count, 0)
        g = g.reshape(parts, owners, size, breadth).transpose(1, 0, 2, 3)
        g_cols = g.reshape(PD, breadth)
    with jax.named_scope("gather_diagonal"):
        g, parts, size = spread_pieces(g_rows[0:tile, :], "row", owners, row_count, 0)
        g = g.reshape(parts, owners, size, PD).transpose(1, 0, 2, 3)
        diag = g.reshape(PD, PD)

    with jax.named_scope("factor_diagonal"):
        eye = jnp.eye(PW, dtype=jnp.float32)
        l11 = jnp.linalg.cholesky(diag[0:PW, 0:PW])
        w0 = lax.linalg.triangular_solve(l11, eye, left_side=True, lower=True).T
        l21 = jnp.dot(diag[PW:PD, 0:PW], w0, precision=HI)
        d22 = diag[PW:PD, PW:PD] - jnp.dot(l21, l21.T, precision=HI)
        l22 = jnp.linalg.cholesky(d22)
        w1 = lax.linalg.triangular_solve(l22, eye, left_side=True, lower=True).T

    def panel_rows(block, gidx):
        s0 = jnp.dot(block[:, 0:PW], w0, precision=HI)
        p0 = jnp.where(
            (gidx >= PW)[:, None], s0, jnp.take(l11, jnp.clip(gidx, 0, PW - 1), axis=0)
        )
        a1 = block[:, PW:PD] - jnp.dot(p0, l21.T, precision=HI)
        s1 = jnp.dot(a1, w1, precision=HI)
        in1 = (gidx >= PW) & (gidx < PD)
        p1 = jnp.where(
            (gidx >= PD)[:, None],
            s1,
            jnp.where(in1[:, None], jnp.take(l22, jnp.clip(gidx - PW, 0, PW - 1), axis=0), 0.0),
        )
        return jnp.concatenate([p0, p1], axis=1)

    with jax.named_scope("panel_factors"):
        pr = panel_rows(g_rows, row_global)
        pc = panel_rows(g_cols.T, col_global)

    with jax.named_scope("trailing_update"):
        out = a2 - jnp.dot(pr, pc.T, precision=HI)
        own = lax.dynamic_slice_in_dim(pr, jnp.minimum(col_index, owners - 1) * tile, tile, axis=1)
        first = jnp.where(col_index < owners, own, out[:, 0:tile])
        out = out.at[:, 0:tile].set(first)
        upper = (row_global[:, None] < PD) & (col_global[None, :] >= PD)
        out = jnp.where(upper, 0.0, out)
    return out.reshape(slots_r, tile, slots_c, tile)


def solution(mesh):
    placed = (P(None, "row", None, "col"), P(None, None, "row", None, "col"), P())
    row_count = mesh.shape["row"]
    col_count = mesh.shape["col"]

    def body(front_blocks, child_updates, child_map):
        return on_device(front_blocks, child_updates, child_map, row_count, col_count)

    return jax.shard_map(
        body,
        mesh=mesh,
        in_specs=placed,
        out_specs=P(None, "row", None, "col"),
        check_vma=False,
    )
```

time: 1380 us -> 810 us (0.59)
  waiting for transfers between devices: 759 us -> 223 us
  local copies, waits for them, and re-layouts: 364 us -> 213 us
  loops' own time: 0.1 us -> 70.7 us
  starting transfers between devices: 15.2 us -> 78.1 us
  other arithmetic: 176 us -> 137 us
  between operations: 16.9 us -> 35.8 us
    psum x6 -> x0, waiting for transfers between devices: 425 us -> none  [the longest x2 185 us: on_device(): panel_rows = lax.psum(jnp.concatenate(pieces, axis=1), 'col')]
    all_to_all x2 -> x0, waiting for transfers between devices: 334 us -> none  [the longest x1 263 us: move_columns(): lax.all_to_all(outgoing, 'col', split_axis=2, concat_axis=2, tiled=True)]
    ppermute x0 -> x29, waiting for transfers between devices: none -> 162 us  [the longest x24 145 us: run(): lax.ppermute(pk[q], axis, [(j, (sigma + q - j) % devices) for j in range(...]
    select_n x6 -> x1, local copies, waits for them, and re-layouts: 93.8 us -> 0.1 us  [decode_map(): order = (shift - start[:, None]) % lanes]
    ppermute x0 -> x29, starting transfers between devices: none -> 77.8 us  [the longest x24 62.9 us: run(): lax.ppermute(pk[q], axis, [(j, (sigma + q - j) % devices) for j in range(...]
    another operation x2 -> x6, loops' own time: 0.1 us -> 70.7 us  [the longest x4 70.6 us: routed(): lax.switch(start % devices, [branch(sg) for sg in range(devices)], *packets)]
    all_gather x0 -> x3, waiting for transfers between devices: none -> 60.8 us  [spread_pieces(): return (lax.all_gather(sub, axis, axis=0, tiled=False), parts, size)]
    gather x15 -> x16, local copies, waits for them, and re-layouts: 99.8 us -> 50.3 us  [the longest x4 16.7 us: panel_rows(): jnp.take(l22, jnp.clip(gidx - PW, 0, PW - 1), axis=0)]
  transfers between devices with their start and end apart: 8 -> 32, of which waited for: 8 -> 24; matrix products, arithmetic and copies ran while one was open for 2% -> 5% of each run, Pallas kernels for 0% -> 0%
where the time goes in v1:
time: 810 us; the launch traced here: 797 us
  waiting for transfers between devices  223 us (28%)
  local copies, waits for them, and re-layouts  213 us (26%)
  other arithmetic  137 us (17%)
  starting transfers between devices  78.1 us (10%)
  loops' own time  70.7 us (9%)
  matrix products  39.7 us (5%)
  between operations  35.8 us (4%)
    ppermute x24, waiting for transfers between devices, run(): lax.ppermute(pk[q], axis, [(j, (sigma + q - j) % devices) for j in range(...  145 us
    another operation x4, loops' own time, routed(): lax.switch(start % devices, [branch(sg) for sg in range(devices)], *packets)  70.6 us
    ppermute x24, starting transfers between devices, run(): lax.ppermute(pk[q], axis, [(j, (sigma + q - j) % devices) for j in range(...  62.9 us
    all_gather x3, waiting for transfers between devices, spread_pieces(): return (lax.all_gather(sub, axis, axis=0, tiled=False), parts, size)  60.8 us
    unnamed x76, local copies, waits for them, and re-layouts  44.1 us
    another operation x7, other arithmetic, on_device(): l22 = jnp.linalg.cholesky(d22)  34.8 us
    another operation x7, other arithmetic, on_device(): l11 = jnp.linalg.cholesky(diag[0:PW, 0:PW])  34.7 us
    another operation x2, local copies, waits for them, and re-layouts, on_device(): y = jnp.stack(got, axis=2)  28.1 us
  transfers between devices with their start and end apart: 32, of which 24 were waited for; matrix products, arithmetic and copies ran while one was open for 5% of the time, Pallas kernels for 0%

profile of v1, /device:TPU:1, one launch (start us, length us, event | category | flops | bytes accessed | tf_op | source)
XLA Modules:
  0.0 797.4 jit_solution(4346453805147752089)
XLA Ops:
  30.8 6.5 fusion.90
  40.3 97.1 %conditional.4 = (bf16[12,128,1,128]{3,2,1,0:T(2,128)(2,1)S(1)}, bf16[12,128,1,128]{3,2,1,0:T(2,128)(2,1)S(1)}, bf16[12,128,1,128]{3,2,1,0:T(2,128)(2,1)S(1)}, b...) conditional(s32[]{:T(128)} %clamp.17, (s32[]{:T(128)}, ...), branch_computations={%region_3.4_spmd, %region_4.5_spmd, %region_5.6_spmd, %region_6.7_... | conditional | flops 18 | bytes 23593476 | solution.py:40
  52.7 5.2 collective-permute-start.54
  57.8 5.9 collective-permute-start.55
  68.4 4.6 collective-permute-start.59
  73.7 5.5 collective-permute-done.55
  79.9 7.3 collective-permute-done.56
  88.0 4.8 collective-permute-done.57
  93.4 7.7 collective-permute-done.58
  101.8 11.8 %collective-permute-done.59 = bf16[12,128,128]{2,1,0:T(8,128)(2,1)S(1)} collective-permute-done((bf16[12,128,128]{2,1,0:T(8,128)(2,1)S(1)}, bf16[12,128,128]{2,1,0:T(8,128)(2,1)S(1)}, u32[]{:S(2)}, u32[]{:S(2)}) %collective-permute-start.59) | collective-permute-done | bytes 393248 | tf_op jit(solution)/shard_map/child_route_cols/cond/branch_9_fun/ppermute | solution.py:32
  139.7 14.1 %stack.910 = bf16[12,128,6,128]{3,2,1,0:T(8,128)(2,1)S(1)} concatenate(bf16[12,128,1,128]{3,2,1,0:T(2,128)(2,1)} %copy-done.5, bf16[12,128,1,128]{3,2,1,0:T(2,128)(2,1)} %copy-done.7, bf16[12,128,1,128]{3,2,1,0:T(2,128)(2,1)} %copy-done.9, bf16[12,128,1,128]{3,2,1,0:T(2,128)(2,1)} %copy-done.11, bf16[12,128,1,128]{3,2,1,0:T(2,128)(2,1)} %copy-done.13, ...), dimensions={2} | concatenate | bytes 4718592 | tf_op jit(solution)/shard_map/child_route_cols/stack | solution.py:71
  153.7 54.1 %conditional.5 = (bf16[1,2,128,6,128]{4,3,2,1,0:T(8,128)(2,1)}, bf16[1,2,128,6,128]{4,3,2,1,0:T(8,128)(2,1)}, bf16[1,2,128,6,128]{4,3,2,1,0:T(8,128)(2,1)}, bf16...) conditional(s32[]{:T(128)} %clamp.16, (s32[]{:T(128)}, ...), branch_computations={%region_19.20_spmd, %region_20.21_spmd, %region_21.22_spmd, %regio... | conditional | flops 18 | bytes 14156292 | solution.py:40
  159.9 3.6 collective-permute-start.105
  166.7 4.3 collective-permute-start.107
  171.0 22.2 %collective-permute-done.104 = bf16[2,128,6,128]{3,2,1,0:T(8,128)(2,1)} collective-permute-done((bf16[2,128,6,128]{3,2,1,0:T(8,128)(2,1)S(1)}, bf16[2,128,6,128]{3,2,1,0:T(8,128)(2,1)}, u32[]{:S(2)}, u32[]{:S(2)}) %collective-permute-start.104) | collective-permute-done | bytes 393248 | tf_op jit(solution)/shard_map/child_route_rows/cond/branch_1_fun/ppermute | solution.py:32
  193.3 5.1 collective-permute-done.105
  198.4 9.2 %collective-permute-done.106 = bf16[2,128,6,128]{3,2,1,0:T(8,128)(2,1)} collective-permute-done((bf16[2,128,6,128]{3,2,1,0:T(8,128)(2,1)S(1)}, bf16[2,128,6,128]{3,2,1,0:T(8,128)(2,1)}, u32[]{:S(2)}, u32[]{:S(2)}) %collective-permute-start.106) | collective-permute-done | bytes 393248 | tf_op jit(solution)/shard_map/child_route_rows/cond/branch_1_fun/ppermute | solution.py:32
  231.3 97.1 %conditional.6 = (bf16[12,128,1,128]{3,2,1,0:T(2,128)(2,1)S(1)}, bf16[12,128,1,128]{3,2,1,0:T(2,128)(2,1)S(1)}, bf16[12,128,1,128]{3,2,1,0:T(2,128)(2,1)S(1)}, b...) conditional(s32[]{:T(128)} %clamp.19, (s32[]{:T(128)}, ...), branch_computations={%region_29.32_spmd, %region_30.33_spmd, %region_31.34_spmd, %regio... | conditional | flops 18 | bytes 23593476 | solution.py:40
  237.7 5.0 collective-permute-start.146
  243.1 4.0 collective-permute-start.148
  247.1 4.8 collective-permute-start.149
  252.6 4.7 collective-permute-done.145
  261.2 3.7 collective-permute-done.147
  265.6 14.0 %collective-permute-done.148 = bf16[12,128,128]{2,1,0:T(8,128)(2,1)S(1)} collective-permute-done((bf16[12,128,128]{2,1,0:T(8,128)(2,1)S(1)}, bf16[12,128,128]{2,1,0:T(8,128)(2,1)S(1)}, u32[]{:S(2)}, u32[]{:S(2)}) %collective-permute-start.148) | collective-permute-done | bytes 393248 | tf_op jit(solution)/shard_map/child_route_cols/cond/branch_0_fun/ppermute | solution.py:32
  280.3 7.7 collective-permute-done.149
  330.6 14.1 %stack.913 = bf16[12,128,6,128]{3,2,1,0:T(8,128)(2,1)S(1)} concatenate(bf16[12,128,1,128]{3,2,1,0:T(2,128)(2,1)} %copy-done.6, bf16[12,128,1,128]{3,2,1,0:T(2,128)(2,1)} %copy-done.8, bf16[12,128,1,128]{3,2,1,0:T(2,128)(2,1)} %copy-done.10, bf16[12,128,1,128]{3,2,1,0:T(2,128)(2,1)} %copy-done.12, bf16[12,128,1,128]{3,2,1,0:T(2,128)(2,1)} %copy-done.14, ...), dimensions={2} | concatenate | bytes 4718592 | tf_op jit(solution)/shard_map/child_route_cols/stack | solution.py:71
  344.6 51.5 %conditional.7 = (bf16[1,2,128,6,128]{4,3,2,1,0:T(8,128)(2,1)}, bf16[1,2,128,6,128]{4,3,2,1,0:T(8,128)(2,1)}, bf16[1,2,128,6,128]{4,3,2,1,0:T(8,128)(2,1)}, bf16...) conditional(s32[]{:T(128)} %clamp.18, (s32[]{:T(128)}, ...), branch_computations={%region_45.48_spmd, %region_46.49_spmd, %region_47.50_spmd, %regio... | conditional | flops 18 | bytes 14156292 | solution.py:40
  348.9 4.0 collective-permute-start.243
  356.6 13.4 %collective-permute-done.240 = bf16[2,128,6,128]{3,2,1,0:T(8,128)(2,1)} collective-permute-done((bf16[2,128,6,128]{3,2,1,0:T(8,128)(2,1)S(1)}, bf16[2,128,6,128]{3,2,1,0:T(8,128)(2,1)}, u32[]{:S(2)}, u32[]{:S(2)}) %collective-permute-start.240) | collective-permute-done | bytes 393248 | tf_op jit(solution)/shard_map/child_route_rows/cond/branch_0_fun/ppermute | solution.py:32
  370.0 16.4 %collective-permute-done.243 = bf16[2,128,6,128]{3,2,1,0:T(8,128)(2,1)} collective-permute-done((bf16[2,128,6,128]{3,2,1,0:T(8,128)(2,1)S(1)}, bf16[2,128,6,128]{3,2,1,0:T(8,128)(2,1)}, u32[]{:S(2)}, u32[]{:S(2)}) %collective-permute-start.243) | collective-permute-done | bytes 393248 | tf_op jit(solution)/shard_map/child_route_rows/cond/branch_0_fun/ppermute | solution.py:32
  386.3 3.9 collective-permute-done.244
  390.2 5.5 collective-permute-done.245
  411.4 5.2 gather_fusion.5
  416.6 5.2 gather_fusion.7
  421.8 9.6 %fusion = f32[16,128,8,128]{3,1,0,2:T(8,128)} fusion(f32[16,128,8,128]{3,2,1,0:T(8,128)} %param.64, bf16[8,16,128,128]{3,2,1,0:T(8,128)(2,1)} %gather_fusion.7, bf16[8,16,128,128]{3,2,1,0:T(8,128)(2,1)} %gather_fusion.5, pred[8]{0:T(512)(128)(4,1)S(1)} %get-tuple-element.4661, pred[8]{0:T(512)(128)(4,1)S(1)} %get-tuple-element.5003), kind=kLoop, calls=%fused_computation.306 | loop fusion | flops 12582912 | bytes 25165840 | tf_op jit(solution)/shard_map/assemble/add | solution.py:116
  431.3 9.1 %copy.214 = f32[16,128,8,128]{1,0,3,2:T(8,128)} copy(f32[16,128,8,128]{3,1,0,2:T(8,128)} %fusion) | data formatting | bytes 16777216 | tf_op jit(solution)/shard_map/assemble/add | solution.py:116
  440.5 7.5 copy.444
  463.0 4.3 collective-permute-done.290
  474.2 5.7 collective-permute-done.292
  480.9 43.2 %all-gather.7.cloned.1.call-done = f32[8192,128]{0,1:T(8,128)} async-done(((f32[512,128]{0,1:T(8,128)}), f32[8192,128]{0,1:T(8,128)}) %all-gather.7.cloned.1.call-update) | async-done | bytes 4194320 | tf_op jit(solution)/shard_map/gather_panel_rows/all_gather | solution.py:52
  524.1 6.0 reshape.626
  530.1 7.4 copy.215
  537.5 4.6 copy.445
  543.0 4.5 collective-permute-start.291
  559.6 17.6 %all-gather.9.cloned.1.call-done = f32[512,512]{1,0:T(8,128)} async-done(((f32[64,512]{1,0:T(8,128)}), f32[512,512]{1,0:T(8,128)}) %all-gather.9.cloned.1.call-update) | async-done | bytes 1048592 | tf_op jit(solution)/shard_map/gather_diagonal/all_gather | solution.py:52
  578.9 11.7 %cholesky.130 = f32[128,128]{1,0:T(8,128)S(1)} custom-call(f32[128,128]{1,0:T(8,128)S(1)} %cholesky.194), custom_call_target="Cholesky" | custom-call | tf_op jit(solution)/shard_map/factor_diagonal/jit(cholesky)/cholesky | solution.py:142
  590.6 9.8 %custom-call.21 = f32[1,128,128]{1,2,0:T(8,128)S(1)} custom-call(f32[1,128,128]{2,1,0:T(8,128)S(1)} %get-tuple-element.4977), custom_call_target="InvertDiagBlocksLowerTriangular" | custom-call | tf_op jit(solution)/shard_map/factor_diagonal/jit(cholesky)/cholesky | solution.py:142
  600.9 11.7 %cholesky.147 = f32[128,128]{1,0:T(8,128)S(1)} custom-call(f32[128,128]{1,0:T(8,128)S(1)} %convolution_subtract_fusion.6), custom_call_target="Cholesky" | custom-call | tf_op jit(solution)/shard_map/factor_diagonal/jit(cholesky)/cholesky | solution.py:142
  615.4 3.9 while.5
  619.4 20.1 %custom-call.22 = f32[2,128,128]{1,2,0:T(8,128)S(1)} custom-call(f32[2,128,128]{2,1,0:T(8,128)S(1)} %get-tuple-element.3949), custom_call_target="InvertDiagBlocksLowerTriangular" | custom-call | tf_op jit(solution)/shard_map/factor_diagonal/triangular_solve/custom-call.0 | solution.py:143
  648.7 4.1 convolution_subtract_fusion.1
  653.4 11.7 %cholesky.164 = f32[128,128]{1,0:T(8,128)S(1)} custom-call(f32[128,128]{1,0:T(8,128)S(1)} %cholesky.197), custom_call_target="Cholesky" | custom-call | tf_op jit(solution)/shard_map/factor_diagonal/jit(cholesky)/cholesky | solution.py:146
  665.2 9.8 %custom-call.23 = f32[1,128,128]{1,2,0:T(8,128)S(1)} custom-call(f32[1,128,128]{2,1,0:T(8,128)S(1)} %get-tuple-element.4973), custom_call_target="InvertDiagBlocksLowerTriangular" | custom-call | tf_op jit(solution)/shard_map/factor_diagonal/jit(cholesky)/cholesky | solution.py:146
  675.4 11.9 %cholesky.181 = f32[128,128]{1,0:T(8,128)S(1)} custom-call(f32[128,128]{1,0:T(8,128)S(1)} %convolution_subtract_fusion.5), custom_call_target="Cholesky" | custom-call | tf_op jit(solution)/shard_map/factor_diagonal/jit(cholesky)/cholesky | solution.py:146
  690.1 4.2 while.6
  694.3 19.7 %custom-call.24 = f32[2,128,128]{1,2,0:T(8,128)S(1)} custom-call(f32[2,128,128]{2,1,0:T(8,128)S(1)} %get-tuple-element.3950), custom_call_target="InvertDiagBlocksLowerTriangular" | custom-call | tf_op jit(solution)/shard_map/factor_diagonal/triangular_solve/custom-call.0 | solution.py:147
  714.9 4.0 gather_fusion.11
  720.2 8.6 %gather_fusion.9 = f32[2048,256]{1,0:T(8,128)} fusion(f32[256,256]{1,0:T(8,128)S(1)} %get-tuple-element.4656, s32[2048]{0:T(1024)S(1)} %get-tuple-element.5010), kind=kCustom, calls=%fused_computation.6.clone | custom fusion | bytes 4202496 | tf_op jit(solution)/shard_map/panel_factors/jit(_take)/gather | solution.py:160
  731.7 8.6 %gather_fusion.8 = f32[2048,256]{1,0:T(8,128)} fusion(f32[256,256]{1,0:T(8,128)S(1)} %get-tuple-element.4658, s32[2048]{0:T(1024)S(1)} %get-tuple-element.5009), kind=kCustom, calls=%fused_computation.2.clone | custom fusion | bytes 4202496 | tf_op jit(solution)/shard_map/panel_factors/jit(_take)/gather | solution.py:152
  743.2 4.3 convolution_select_fusion.1
  747.5 5.2 convolution_subtract_fusion
  756.5 16.1 %fusion.2 = f32[2048,1024]{0,1:T(8,128)S(1)} fusion(f32[2048,256]{0,1:T(8,128)S(1)} %convolution_select_fusion, f32[2048,256]{0,1:T(8,128)S(1)} %convolution_select_fusion.1, f32[1024,256]{0,1:T(8,128)S(1)} %convolution_select_fusion.2, f32[1024,256]{0,1:T(8,128)S(1)} %convolution_select_fusion.3, f32[128,8,16,128]{3,2,1,0:T(8,128)S(1)} %bitcast.502), kind=kOutput, calls=%fused_computation.313 | convolution fusion | flops 12888571904 | bytes 23068672 | tf_op jit(solution)/shard_map/trailing_update/dot_general | solution.py:169
  774.7 5.3 copy.434
  780.0 10.7 %copy.231 = f32[16,128,8,128]{3,2,1,0:T(8,128)} copy(f32[16,128,8,128]{1,0,3,2:T(8,128)} %bitcast.503) | data formatting | bytes 16777216 | tf_op jit(solution)/shard_map/reshape | solution.py:175
  (250 shorter events, 168.8 us)
Async XLA Ops:
  6.5 517.6 %all-gather.7.cloned.1.call-start = ((), (), s32[]{:S(2)}) async-start(), calls=%async_computation | async-start | bytes 4456448 | tf_op jit(solution)/shard_map/gather_panel_rows/all_gather | solution.py:52
  52.7 15.7 %collective-permute-start.54 = (bf16[12,128,128]{2,1,0:T(8,128)(2,1)S(1)}, bf16[12,128,128]{2,1,0:T(8,128)(2,1)S(1)}, u32[]{:S(2)}, u32[]{:S(2)}) collective-permute-start(bf16[12,128,128]{2,1,0:T(8,128)(2,1)S(1)} %get-tuple-element.4728), channel_id=1, source_target_pairs={{0,9},{1,8},{2,7},{3,6},{4,5},{5,4},{6,3},{7,2},{8,1},{9,0},{10,15... | collective-permute-start | bytes 1179656 | tf_op jit(solution)/shard_map/child_route_cols/cond/branch_9_fun/ppermute | solution.py:32
  57.8 21.4 %collective-permute-start.55 = (bf16[12,128,128]{2,1,0:T(8,128)(2,1)S(1)}, bf16[12,128,128]{2,1,0:T(8,128)(2,1)S(1)}, u32[]{:S(2)}, u32[]{:S(2)}) collective-permute-start(bf16[12,128,128]{2,1,0:T(8,128)(2,1)S(1)} %get-tuple-element.4727), channel_id=1, source_target_pairs={{0,10},{1,9},{2,8},{3,7},{4,6},{5,5},{6,4},{7,3},{8,2},{9,1},{10,0... | collective-permute-start | bytes 1179656 | tf_op jit(solution)/shard_map/child_route_cols/cond/branch_9_fun/ppermute | solution.py:32
  63.8 23.5 %collective-permute-start.56 = (bf16[12,128,128]{2,1,0:T(8,128)(2,1)S(1)}, bf16[12,128,128]{2,1,0:T(8,128)(2,1)S(1)}, u32[]{:S(2)}, u32[]{:S(2)}) collective-permute-start(bf16[12,128,128]{2,1,0:T(8,128)(2,1)S(1)} %get-tuple-element.4726), channel_id=1, source_target_pairs={{0,11},{1,10},{2,9},{3,8},{4,7},{5,6},{6,5},{7,4},{8,3},{9,2},{10,... | collective-permute-start | bytes 1179656 | tf_op jit(solution)/shard_map/child_route_cols/cond/branch_9_fun/ppermute | solution.py:32
  63.9 28.9 %collective-permute-start.57 = (bf16[12,128,128]{2,1,0:T(8,128)(2,1)S(1)}, bf16[12,128,128]{2,1,0:T(8,128)(2,1)S(1)}, u32[]{:S(2)}, u32[]{:S(2)}) collective-permute-start(bf16[12,128,128]{2,1,0:T(8,128)(2,1)S(1)} %get-tuple-element.4725), channel_id=1, source_target_pairs={{0,12},{1,11},{2,10},{3,9},{4,8},{5,7},{6,6},{7,5},{8,4},{9,3},{10... | collective-permute-start | bytes 1179656 | tf_op jit(solution)/shard_map/child_route_cols/cond/branch_9_fun/ppermute | solution.py:32
  65.8 35.3 %collective-permute-start.58 = (bf16[12,128,128]{2,1,0:T(8,128)(2,1)S(1)}, bf16[12,128,128]{2,1,0:T(8,128)(2,1)S(1)}, u32[]{:S(2)}, u32[]{:S(2)}) collective-permute-start(bf16[12,128,128]{2,1,0:T(8,128)(2,1)S(1)} %get-tuple-element.4724), channel_id=1, source_target_pairs={{0,13},{1,12},{2,11},{3,10},{4,9},{5,8},{6,7},{7,6},{8,5},{9,4},{1... | collective-permute-start | bytes 1179656 | tf_op jit(solution)/shard_map/child_route_cols/cond/branch_9_fun/ppermute | solution.py:32
  68.4 45.2 %collective-permute-start.59 = (bf16[12,128,128]{2,1,0:T(8,128)(2,1)S(1)}, bf16[12,128,128]{2,1,0:T(8,128)(2,1)S(1)}, u32[]{:S(2)}, u32[]{:S(2)}) collective-permute-start(bf16[12,128,128]{2,1,0:T(8,128)(2,1)S(1)} %get-tuple-element.4723), channel_id=1, source_target_pairs={{0,14},{1,13},{2,12},{3,11},{4,10},{5,9},{6,8},{7,7},{8,6},{9,5},{... | collective-permute-start | bytes 1179656 | tf_op jit(solution)/shard_map/child_route_cols/cond/branch_9_fun/ppermute | solution.py:32
  137.5 0.9 copy-start.5
  137.5 1.2 copy-start.7
  137.5 1.4 copy-start.9
  137.5 1.6 copy-start.11
  137.5 1.9 copy-start.13
  137.5 2.1 copy-start.15
  154.5 12.1 %collective-permute-start.102 = (bf16[2,128,6,128]{3,2,1,0:T(8,128)(2,1)S(1)}, bf16[2,128,6,128]{3,2,1,0:T(8,128)(2,1)}, u32[]{:S(2)}, u32[]{:S(2)}) collective-permute-start(bf16[2,128,6,128]{3,2,1,0:T(8,128)(2,1)S(1)} %get-tuple-element.4776), channel_id=1, source_target_pairs={{0,16},{16,0},{32,112},{48,96},{64,80},{80,64},{96,48},{112,32},{1... | collective-permute-start | bytes 1179656 | tf_op jit(solution)/shard_map/child_route_rows/cond/branch_1_fun/ppermute | solution.py:32
  155.1 15.9 %collective-permute-start.103 = (bf16[2,128,6,128]{3,2,1,0:T(8,128)(2,1)S(1)}, bf16[2,128,6,128]{3,2,1,0:T(8,128)(2,1)}, u32[]{:S(2)}, u32[]{:S(2)}) collective-permute-start(bf16[2,128,6,128]{3,2,1,0:T(8,128)(2,1)S(1)} %get-tuple-element.4775), channel_id=1, source_target_pairs={{0,32},{16,16},{32,0},{48,112},{64,96},{80,80},{96,64},{112,48},{1... | collective-permute-start | bytes 1179656 | tf_op jit(solution)/shard_map/child_route_rows/cond/branch_1_fun/ppermute | solution.py:32
  156.5 36.8 %collective-permute-start.104 = (bf16[2,128,6,128]{3,2,1,0:T(8,128)(2,1)S(1)}, bf16[2,128,6,128]{3,2,1,0:T(8,128)(2,1)}, u32[]{:S(2)}, u32[]{:S(2)}) collective-permute-start(bf16[2,128,6,128]{3,2,1,0:T(8,128)(2,1)S(1)} %get-tuple-element.4774), channel_id=1, source_target_pairs={{0,48},{16,32},{32,16},{48,0},{64,112},{80,96},{96,80},{112,64},{1... | collective-permute-start | bytes 1179656 | tf_op jit(solution)/shard_map/child_route_rows/cond/branch_1_fun/ppermute | solution.py:32
  159.9 38.5 %collective-permute-start.105 = (bf16[2,128,6,128]{3,2,1,0:T(8,128)(2,1)S(1)}, bf16[2,128,6,128]{3,2,1,0:T(8,128)(2,1)}, u32[]{:S(2)}, u32[]{:S(2)}) collective-permute-start(bf16[2,128,6,128]{3,2,1,0:T(8,128)(2,1)S(1)} %get-tuple-element.4773), channel_id=1, source_target_pairs={{0,64},{16,48},{32,32},{48,16},{64,0},{80,112},{96,96},{112,80},{1... | collective-permute-start | bytes 1179656 | tf_op jit(solution)/shard_map/child_route_rows/cond/branch_1_fun/ppermute | solution.py:32
  163.6 44.1 %collective-permute-start.106 = (bf16[2,128,6,128]{3,2,1,0:T(8,128)(2,1)S(1)}, bf16[2,128,6,128]{3,2,1,0:T(8,128)(2,1)}, u32[]{:S(2)}, u32[]{:S(2)}) collective-permute-start(bf16[2,128,6,128]{3,2,1,0:T(8,128)(2,1)S(1)} %get-tuple-element.4772), channel_id=1, source_target_pairs={{0,80},{16,64},{32,48},{48,32},{64,16},{80,0},{96,112},{112,96},{1... | collective-permute-start | bytes 1179656 | tf_op jit(solution)/shard_map/child_route_rows/cond/branch_1_fun/ppermute | solution.py:32
  166.7 41.0 %collective-permute-start.107 = (bf16[2,128,6,128]{3,2,1,0:T(8,128)(2,1)S(1)}, bf16[2,128,6,128]{3,2,1,0:T(8,128)(2,1)}, u32[]{:S(2)}, u32[]{:S(2)}) collective-permute-start(bf16[2,128,6,128]{3,2,1,0:T(8,128)(2,1)S(1)} %get-tuple-element.4771), channel_id=1, source_target_pairs={{0,96},{16,80},{32,64},{48,48},{64,32},{80,16},{96,0},{112,112},{1... | collective-permute-start | bytes 1179656 | tf_op jit(solution)/shard_map/child_route_rows/cond/branch_1_fun/ppermute | solution.py:32
  236.9 10.2 %collective-permute-start.144 = (bf16[12,128,128]{2,1,0:T(8,128)(2,1)S(1)}, bf16[12,128,128]{2,1,0:T(8,128)(2,1)S(1)}, u32[]{:S(2)}, u32[]{:S(2)}) collective-permute-start(bf16[12,128,128]{2,1,0:T(8,128)(2,1)S(1)} %get-tuple-element.4818), channel_id=1, source_target_pairs={{0,0},{1,15},{2,14},{3,13},{4,12},{5,11},{6,10},{7,9},{8,8},{9,7},... | collective-permute-start | bytes 1179656 | tf_op jit(solution)/shard_map/child_route_cols/cond/branch_0_fun/ppermute | solution.py:32
  237.6 19.7 %collective-permute-start.145 = (bf16[12,128,128]{2,1,0:T(8,128)(2,1)S(1)}, bf16[12,128,128]{2,1,0:T(8,128)(2,1)S(1)}, u32[]{:S(2)}, u32[]{:S(2)}) collective-permute-start(bf16[12,128,128]{2,1,0:T(8,128)(2,1)S(1)} %get-tuple-element.4817), channel_id=1, source_target_pairs={{0,1},{1,0},{2,15},{3,14},{4,13},{5,12},{6,11},{7,10},{8,9},{9,8},... | collective-permute-start | bytes 1179656 | tf_op jit(solution)/shard_map/child_route_cols/cond/branch_0_fun/ppermute | solution.py:32
  237.7 22.8 %collective-permute-start.146 = (bf16[12,128,128]{2,1,0:T(8,128)(2,1)S(1)}, bf16[12,128,128]{2,1,0:T(8,128)(2,1)S(1)}, u32[]{:S(2)}, u32[]{:S(2)}) collective-permute-start(bf16[12,128,128]{2,1,0:T(8,128)(2,1)S(1)} %get-tuple-element.4816), channel_id=1, source_target_pairs={{0,2},{1,1},{2,0},{3,15},{4,14},{5,13},{6,12},{7,11},{8,10},{9,9},... | collective-permute-start | bytes 1179656 | tf_op jit(solution)/shard_map/child_route_cols/cond/branch_0_fun/ppermute | solution.py:32
  242.7 22.2 %collective-permute-start.147 = (bf16[12,128,128]{2,1,0:T(8,128)(2,1)S(1)}, bf16[12,128,128]{2,1,0:T(8,128)(2,1)S(1)}, u32[]{:S(2)}, u32[]{:S(2)}) collective-permute-start(bf16[12,128,128]{2,1,0:T(8,128)(2,1)S(1)} %get-tuple-element.4815), channel_id=1, source_target_pairs={{0,3},{1,2},{2,1},{3,0},{4,15},{5,14},{6,13},{7,12},{8,11},{9,10},... | collective-permute-start | bytes 1179656 | tf_op jit(solution)/shard_map/child_route_cols/cond/branch_0_fun/ppermute | solution.py:32
  243.1 36.5 %collective-permute-start.148 = (bf16[12,128,128]{2,1,0:T(8,128)(2,1)S(1)}, bf16[12,128,128]{2,1,0:T(8,128)(2,1)S(1)}, u32[]{:S(2)}, u32[]{:S(2)}) collective-permute-start(bf16[12,128,128]{2,1,0:T(8,128)(2,1)S(1)} %get-tuple-element.4814), channel_id=1, source_target_pairs={{0,4},{1,3},{2,2},{3,1},{4,0},{5,15},{6,14},{7,13},{8,12},{9,11},{... | collective-permute-start | bytes 1179656 | tf_op jit(solution)/shard_map/child_route_cols/cond/branch_0_fun/ppermute | solution.py:32
  247.1 41.0 %collective-permute-start.149 = (bf16[12,128,128]{2,1,0:T(8,128)(2,1)S(1)}, bf16[12,128,128]{2,1,0:T(8,128)(2,1)S(1)}, u32[]{:S(2)}, u32[]{:S(2)}) collective-permute-start(bf16[12,128,128]{2,1,0:T(8,128)(2,1)S(1)} %get-tuple-element.4813), channel_id=1, source_target_pairs={{0,5},{1,4},{2,3},{3,2},{4,1},{5,0},{6,15},{7,14},{8,13},{9,12},{1... | collective-permute-start | bytes 1179656 | tf_op jit(solution)/shard_map/child_route_cols/cond/branch_0_fun/ppermute | solution.py:32
  328.4 0.9 copy-start.6
  328.4 1.2 copy-start.8
  328.4 1.4 copy-start.10
  328.4 1.7 copy-start.12
  328.4 1.9 copy-start.14
  328.4 2.1 copy-start.16
  345.4 24.5 %collective-permute-start.240 = (bf16[2,128,6,128]{3,2,1,0:T(8,128)(2,1)S(1)}, bf16[2,128,6,128]{3,2,1,0:T(8,128)(2,1)}, u32[]{:S(2)}, u32[]{:S(2)}) collective-permute-start(bf16[2,128,6,128]{3,2,1,0:T(8,128)(2,1)S(1)} %get-tuple-element.4914), channel_id=1, source_target_pairs={{0,0},{16,112},{32,96},{48,80},{64,64},{80,48},{96,32},{112,16},{1... | collective-permute-start | bytes 1179656 | tf_op jit(solution)/shard_map/child_route_rows/cond/branch_0_fun/ppermute | solution.py:32
  347.3 22.6 %collective-permute-start.241 = (bf16[2,128,6,128]{3,2,1,0:T(8,128)(2,1)S(1)}, bf16[2,128,6,128]{3,2,1,0:T(8,128)(2,1)}, u32[]{:S(2)}, u32[]{:S(2)}) collective-permute-start(bf16[2,128,6,128]{3,2,1,0:T(8,128)(2,1)S(1)} %get-tuple-element.4913), channel_id=1, source_target_pairs={{0,16},{16,0},{32,112},{48,96},{64,80},{80,64},{96,48},{112,32},{1... | collective-permute-start | bytes 1179656 | tf_op jit(solution)/shard_map/child_route_rows/cond/branch_0_fun/ppermute | solution.py:32
  347.4 22.5 %collective-permute-start.242 = (bf16[2,128,6,128]{3,2,1,0:T(8,128)(2,1)S(1)}, bf16[2,128,6,128]{3,2,1,0:T(8,128)(2,1)}, u32[]{:S(2)}, u32[]{:S(2)}) collective-permute-start(bf16[2,128,6,128]{3,2,1,0:T(8,128)(2,1)S(1)} %get-tuple-element.4912), channel_id=1, source_target_pairs={{0,32},{16,16},{32,0},{48,112},{64,96},{80,80},{96,64},{112,48},{1... | collective-permute-start | bytes 1179656 | tf_op jit(solution)/shard_map/child_route_rows/cond/branch_0_fun/ppermute | solution.py:32
  348.9 37.4 %collective-permute-start.243 = (bf16[2,128,6,128]{3,2,1,0:T(8,128)(2,1)S(1)}, bf16[2,128,6,128]{3,2,1,0:T(8,128)(2,1)}, u32[]{:S(2)}, u32[]{:S(2)}) collective-permute-start(bf16[2,128,6,128]{3,2,1,0:T(8,128)(2,1)S(1)} %get-tuple-element.4911), channel_id=1, source_target_pairs={{0,48},{16,32},{32,16},{48,0},{64,112},{80,96},{96,80},{112,64},{1... | collective-permute-start | bytes 1179656 | tf_op jit(solution)/shard_map/child_route_rows/cond/branch_0_fun/ppermute | solution.py:32
  352.9 37.3 %collective-permute-start.244 = (bf16[2,128,6,128]{3,2,1,0:T(8,128)(2,1)S(1)}, bf16[2,128,6,128]{3,2,1,0:T(8,128)(2,1)}, u32[]{:S(2)}, u32[]{:S(2)}) collective-permute-start(bf16[2,128,6,128]{3,2,1,0:T(8,128)(2,1)S(1)} %get-tuple-element.4910), channel_id=1, source_target_pairs={{0,64},{16,48},{32,32},{48,16},{64,0},{80,112},{96,96},{112,80},{1... | collective-permute-start | bytes 1179656 | tf_op jit(solution)/shard_map/child_route_rows/cond/branch_0_fun/ppermute | solution.py:32
  369.9 25.8 %collective-permute-start.245 = (bf16[2,128,6,128]{3,2,1,0:T(8,128)(2,1)S(1)}, bf16[2,128,6,128]{3,2,1,0:T(8,128)(2,1)}, u32[]{:S(2)}, u32[]{:S(2)}) collective-permute-start(bf16[2,128,6,128]{3,2,1,0:T(8,128)(2,1)S(1)} %get-tuple-element.4909), channel_id=1, source_target_pairs={{0,80},{16,64},{32,48},{48,32},{64,16},{80,0},{96,112},{112,96},{1... | collective-permute-start | bytes 1179656 | tf_op jit(solution)/shard_map/child_route_rows/cond/branch_0_fun/ppermute | solution.py:32
  448.0 3.3 copy-start
  451.3 9.0 %collective-permute-start.288 = (f32[512,128]{0,1:T(8,128)S(1)}, f32[512,128]{0,1:T(8,128)S(1)}, u32[]{:S(2)}, u32[]{:S(2)}) collective-permute-start(f32[512,128]{0,1:T(8,128)S(1)} %get-tuple-element.4965), channel_id=1, source_target_pairs={{0,12},{1,13},{2,14},{3,15},{16,28},{17,29},{18,30},{19,31},{32,44... | collective-permute-start | bytes 786440 | tf_op jit(solution)/shard_map/gather_panel_rows/ppermute | solution.py:50
  454.7 8.3 %collective-permute-start.289 = (f32[512,128]{0,1:T(8,128)S(1)}, f32[512,128]{0,1:T(8,128)S(1)}, u32[]{:S(2)}, u32[]{:S(2)}) collective-permute-start(f32[512,128]{0,1:T(8,128)S(1)} %get-tuple-element.4964), channel_id=1, source_target_pairs={{0,8},{1,9},{2,10},{3,11},{16,24},{17,25},{18,26},{19,27},{32,40},... | collective-permute-start | bytes 786440 | tf_op jit(solution)/shard_map/gather_panel_rows/ppermute | solution.py:50
  456.9 10.4 %collective-permute-start.290 = (f32[512,128]{0,1:T(8,128)S(1)}, f32[512,128]{0,1:T(8,128)S(1)}, u32[]{:S(2)}, u32[]{:S(2)}) collective-permute-start(f32[512,128]{0,1:T(8,128)S(1)} %get-tuple-element.4963), channel_id=1, source_target_pairs={{0,4},{1,5},{2,6},{3,7},{16,20},{17,21},{18,22},{19,23},{32,36},{3... | collective-permute-start | bytes 786440 | tf_op jit(solution)/shard_map/gather_panel_rows/ppermute | solution.py:50
  469.1 87.0 %all-gather.11.cloned.1.call-start = ((), (), s32[]{:S(2)}) async-start(), calls=%async_computation.2 | async-start | bytes 2359296 | tf_op jit(solution)/shard_map/gather_panel_cols/all_gather | solution.py:52
  470.4 9.5 %collective-permute-start.292 = (f32[64,1024]{1,0:T(8,128)S(1)}, f32[64,1024]{1,0:T(8,128)S(1)}, u32[]{:S(2)}, u32[]{:S(2)}) collective-permute-start(f32[64,1024]{1,0:T(8,128)S(1)} %bitcast.711), channel_id=1, source_target_pairs={{0,64},{16,80},{32,96},{48,112},{1,65},{17,81},{33,97},{49,113},{2... | collective-permute-start | bytes 786440 | tf_op jit(solution)/shard_map/gather_panel_cols/ppermute | solution.py:50
  480.7 96.6 %all-gather.9.cloned.1.call-start = ((), (), s32[]{:S(2)}) async-start(), calls=%async_computation.1 | async-start | bytes 1179648 | tf_op jit(solution)/shard_map/gather_diagonal/all_gather | solution.py:52
  543.0 6.5 collective-permute-start.291
  578.6 36.7 %copy-start.3 = (f32[4,2,64,512]{3,2,1,0:T(8,128)}, f32[4,2,64,512]{3,2,1,0:T(8,128)S(1)}, u32[]{:S(2)}) copy-start(f32[4,2,64,512]{3,2,1,0:T(8,128)S(1)} %copy.216) | copy-start | bytes 3145732
  648.7 4.1 copy-start.17
  740.3 2.9 copy-start.22
  740.3 2.9 copy-start.23
  747.5 5.3 copy-start.2
  747.5 5.3 copy-start.4
  747.5 5.3 copy-start.24
  747.5 5.3 copy-start.25
  747.5 5.3 copy-start.26
  747.5 8.9 %slice-start = ((s8[8388608]{0:T(1024)(128)(4,1)}), s8[4194304]{0:T(1024)(128)(4,1)S(1)}, s32[]{:S(2)}) async-start(s8[8388608]{0:T(1024)(128)(4,1)} %bitcast.500), calls=%async_computation.3 | async-start | bytes 8388608
  752.7 1.6 copy-start.1
  752.7 1.6 copy-start.19
  752.7 1.6 copy-start.20
  752.8 1.6 copy-start.21
  752.8 3.7 slice-start.1
  772.6 1.1 copy-start.18
Sparse Core Ops, SparseCore 0:
  469.2 54.8 all-gather.6
  525.8 25.1 all-gather.10
  552.7 24.5 all-gather.8

commit v2 on v1

--- a/solution.py
+++ b/solution.py
@@ -1,12 +1,17 @@
+import functools
+
 import jax
 import jax.numpy as jnp
 from jax import lax
+from jax.experimental import pallas as pl
+from jax.experimental.pallas import tpu as pltpu
 from jax.sharding import PartitionSpec as P
 
 PW = 256
 PANELS = 2
 PD = 512
 HI = lax.Precision.HIGHEST
+MESH = pl.DeviceIdType.MESH
 
 
 def decode_map(child_map, lanes):
@@ -23,21 +28,79 @@
     return home, shift, start, inv
 
 
-def routed(packets, axis, devices, start):
-    groups = len(packets)
-
-    def branch(sigma):
-        def run(*pk):
-            return tuple(
-                lax.ppermute(
-                    pk[q], axis, [(j, (sigma + q - j) % devices) for j in range(devices)]
-                )
-                for q in range(groups)
+def route_kernel(axis, devices, sigma, groups, pk_ref, out_ref, send_sem, recv_sem):
+    me = lax.axis_index(axis)
+    row_at = lax.axis_index("row")
+    col_at = lax.axis_index("col")
+
+    def where_to(partner):
+        return (partner, col_at) if axis == "row" else (row_at, partner)
+
+    partners = [lax.rem(sigma + q - me + devices, devices) for q in range(groups)]
+    barrier = pltpu.get_barrier_semaphore()
+    for q in range(groups):
+
+        @pl.when(partners[q] != me)
+        def _():
+            pl.semaphore_signal(barrier, 1, device_id=where_to(partners[q]), device_id_type=MESH)
+
+    peers = sum((p != me).astype(jnp.int32) for p in partners)
+    pl.semaphore_wait(barrier, peers)
+
+    remote = []
+    local = []
+    for q in range(groups):
+        remote.append(
+            pltpu.make_async_remote_copy(
+                src_ref=pk_ref.at[q],
+                dst_ref=out_ref.at[q],
+                send_sem=send_sem.at[q],
+                recv_sem=recv_sem.at[q],
+                device_id=where_to(partners[q]),
+                device_id_type=MESH,
             )
-
-        return run
-
-    return lax.switch(start % devices, [branch(sg) for sg in range(devices)], *packets)
+        )
+        local.append(pltpu.make_async_copy(pk_ref.at[q], out_ref.at[q], recv_sem.at[q]))
+    for q in range(groups):
+
+        @pl.when(partners[q] != me)
+        def _():
+            remote[q].start()
+
+        @pl.when(partners[q] == me)
+        def _():
+            local[q].start()
+
+    for q in range(groups):
+
+        @pl.when(partners[q] != me)
+        def _():
+            remote[q].wait()
+
+        @pl.when(partners[q] == me)
+        def _():
+            local[q].wait()
+
+
+def route_call(packets, axis, devices, sigma, base_id):
+    groups = packets.shape[0]
+    return pl.pallas_call(
+        functools.partial(route_kernel, axis, devices, sigma, groups),
+        out_shape=jax.ShapeDtypeStruct(packets.shape, packets.dtype),
+        in_specs=[pl.BlockSpec(memory_space=pl.ANY)],
+        out_specs=pl.BlockSpec(memory_space=pl.ANY),
+        scratch_shapes=[pltpu.SemaphoreType.DMA((groups,)), pltpu.SemaphoreType.DMA((groups,))],
+        compiler_params=pltpu.CompilerParams(collective_id=base_id + sigma, has_side_effects=True),
+        name=f"route_{axis}_{sigma}",
+    )(packets)
+
+
+def routed(packets, axis, devices, start, base_id):
+    branches = [
+        functools.partial(route_call, axis=axis, devices=devices, sigma=sg, base_id=base_id)
+        for sg in range(devices)
+    ]
+    return lax.switch(start % devices, branches, packets)
 
 
 def spread_pieces(piece, axis, owners, devices, pieces_axis):
@@ -64,17 +127,17 @@
     for i in range(child_count):
         with jax.named_scope("child_route_cols"):
             x = child_updates[i].reshape(kr_count, tile, kc_count * tile)
-            col_packets = [
-                lax.dynamic_slice_in_dim(x, inv[i, q] * tile, tile, axis=2) for q in range(groups)
-            ]
-            got = routed(col_packets, "col", col_count, start[i])
-            y = jnp.stack(got, axis=2)
+            col_packets = jnp.stack(
+                [lax.dynamic_slice_in_dim(x, inv[i, q] * tile, tile, axis=2) for q in range(groups)]
+            )
+            got = routed(col_packets, "col", col_count, start[i], 0)
+            y = jnp.moveaxis(got, 0, 2)
         with jax.named_scope("child_route_rows"):
-            row_packets = [
-                lax.dynamic_slice_in_dim(y, inv[i, q] * 2, 2, axis=0) for q in range(groups)
-            ]
-            got = routed(row_packets, "row", row_count, start[i])
-            z = jnp.stack(got, axis=0).reshape(groups * 2, tile, groups, tile)
+            row_packets = jnp.stack(
+                [lax.dynamic_slice_in_dim(y, inv[i, q] * 2, 2, axis=0) for q in range(groups)]
+            )
+            got = routed(row_packets, "row", row_count, start[i], col_count)
+            z = got.reshape(groups * 2, tile, groups, tile)
         with jax.named_scope("child_place"):
             qs = jnp.arange(groups)
             a_of = inv[i]

time: 810 us -> 800 us (0.988)
  Pallas kernels: 0 us -> 233 us
  waiting for transfers between devices: 223 us -> 77.5 us
  starting transfers between devices: 78.1 us -> 29 us
  loops' own time: 70.7 us -> 32.1 us
  local copies, waits for them, and re-layouts: 213 us -> 204 us
    pallas_call x0 -> x4, Pallas kernels: none -> 233 us  [route_call(): pl.pallas_call(functools.partial(route_kernel, axis, devices, sigma, grou...]
    ppermute x24 -> x0, waiting for transfers between devices: 145 us -> none  [run(): lax.ppermute(pk[q], axis, [(j, (sigma + q - j) % devices) for j in range(...]
    ppermute x24 -> x0, starting transfers between devices: 62.9 us -> none  [run(): lax.ppermute(pk[q], axis, [(j, (sigma + q - j) % devices) for j in range(...]
    another operation x4, loops' own time: 70.6 us -> 32 us  [routed(): return lax.switch(start % devices, branches, packets)]
    another operation x8 -> x4, local copies, waits for them, and re-layouts: 38 us -> 3.91 us  [the longest x2 3.08 us: on_device(): jnp.stack([lax.dynamic_slice_in_dim(y, inv[i, q] * 2, 2, axis=0) for q in...]
    ppermute x5, starting transfers between devices: 14.9 us -> 28.9 us  [spread_pieces(): got = lax.ppermute(part, axis, [(k, m * owners + k) for k in range(owners)])]
    dynamic_slice x2 -> x14, local copies, waits for them, and re-layouts: 6.26 us -> 16.7 us  [on_device(): lax.dynamic_slice_in_dim(x, inv[i, q] * tile, tile, axis=2)]
    unnamed x76 -> x86, local copies, waits for them, and re-layouts: 44.1 us -> 50.8 us
  transfers between devices with their start and end apart: 32 -> 8, of which waited for: 24 -> 6; matrix products, arithmetic and copies ran while one was open for 5% -> 3% of each run, Pallas kernels for 0% -> 0%
where the time goes in v2:
time: 800 us; the launch traced here: 787 us
  Pallas kernels  233 us (29%)
  local copies, waits for them, and re-layouts  204 us (26%)
  other arithmetic  137 us (17%)
  waiting for transfers between devices  77.5 us (10%)
  matrix products  38 us (5%)
  between operations  36.1 us (5%)
  loops' own time  32.1 us (4%)
  starting transfers between devices  29 us (4%)
    pallas_call x4, Pallas kernels, route_call(): pl.pallas_call(functools.partial(route_kernel, axis, devices, sigma, grou...  233 us
    all_gather x3, waiting for transfers between devices, spread_pieces(): return (lax.all_gather(sub, axis, axis=0, tiled=False), parts, size)  60.2 us
    unnamed x86, local copies, waits for them, and re-layouts  50.8 us
    another operation x7, other arithmetic, on_device(): l22 = jnp.linalg.cholesky(d22)  35.1 us
    another operation x7, other arithmetic, on_device(): l11 = jnp.linalg.cholesky(diag[0:PW, 0:PW])  34.6 us
    another operation x4, loops' own time, routed(): return lax.switch(start % devices, branches, packets)  32 us
    ppermute x5, starting transfers between devices, spread_pieces(): got = lax.ppermute(part, axis, [(k, m * owners + k) for k in range(owners)])  28.9 us
    another operation x3, other arithmetic, on_device(): w0 = lax.linalg.triangular_solve(l11, eye, left_side=True, lower=True).T  19.7 us
  transfers between devices with their start and end apart: 8, of which 6 were waited for; matrix products, arithmetic and copies ran while one was open for 3% of the time, Pallas kernels for 0%

profile of v2, /device:TPU:1, one launch (start us, length us, event | category | flops | bytes accessed | tf_op | source)
XLA Modules:
  0.0 787.0 jit_solution(1849597272250827489)
XLA Ops:
  32.3 6.4 fusion.90
  38.7 3.0 copy.224
  55.3 3.0 copy.225
  62.5 2.0 copy.128
  75.6 85.3 %conditional.4 = (bf16[6,12,128,128]{3,0,2,1:T(8,128)(2,1)}) conditional(s32[]{:T(128)} %clamp.17, bf16[6,12,128,128]{3,2,1,0:T(8,128)(2,1)} %bitcast_dynamic-update-slice_fusion.20, bf16[6,12,128,128]{3,2,1,0:T(8,128)(2,1)} %bitcast_dynamic-update-slice_fusion.20, ...), branch_computations={%region_3.4_spmd, %region_4.5_spmd, %region_5.6_spmd, %region_6.7_... | conditional | bytes 4718600 | solution.py:103
  88.5 67.1 %route_col_14.2 = bf16[6,12,128,128]{3,2,1,0:T(8,128)(2,1)} custom-call(bf16[6,12,128,128]{3,2,1,0:T(8,128)(2,1)} %pk_ref.14), custom_call_target="tpu_custom_call" | custom-call | tf_op jit(solution)/shard_map/child_route_cols/cond/branch_14_fun/route_col_14/pallas_call | solution.py:87
  155.6 5.1 copy.174
  162.9 1.9 bitcast_dynamic-update-slice_fusion.12
  172.5 53.1 %conditional.5 = (bf16[13,128,6,128]{3,1,2,0:T(8,128)(2,1)}) conditional(s32[]{:T(128)} %clamp.16, bf16[6,2,128,6,128]{4,3,2,1,0:T(8,128)(2,1)} %bitcast_dynamic-update-slice_fusion.8, bf16[6,2,128,6,128]{4,3,2,1,0:T(8,128)(2,1)} %bitcast_dynamic-update-slice_fusion.8, ...), branch_computations={%region_19.20_spmd, %region_20.21_spmd, %region_21.22_spmd, %regio... | conditional | bytes 9633802 | solution.py:103
  172.5 48.8 %route_row_6.2 = bf16[6,2,128,6,128]{4,3,2,1,0:T(8,128)(2,1)} custom-call(bf16[6,2,128,6,128]{4,3,2,1,0:T(8,128)(2,1)} %pk_ref.22), custom_call_target="tpu_custom_call" | custom-call | tf_op jit(solution)/shard_map/child_route_rows/cond/branch_6_fun/route_row_6/pallas_call | solution.py:87
  221.3 2.5 copy.214
  225.7 4.3 gather_fusion.4
  230.0 2.2 broadcast_select_fusion.1
  232.3 2.4 concatenate.60
  234.9 90.5 %conditional.6 = (bf16[6,12,128,128]{3,0,2,1:T(8,128)(2,1)}) conditional(s32[]{:T(128)} %clamp.19, bf16[6,12,128,128]{3,2,1,0:T(8,128)(2,1)S(1)} %bitcast_dynamic-update-slice_fusion.14, bf16[6,12,128,128]{3,2,1,0:T(8,128)(2,1)S(1)} %bitcast_dynamic-update-slice_fusion.14, ...), branch_computations={%region_29.32_spmd, %region_30.33_spmd, %region_31.34_spmd, %regio... | conditional | bytes 4718600 | solution.py:103
  235.4 66.6 %route_col_2.3 = bf16[6,12,128,128]{3,2,1,0:T(8,128)(2,1)} custom-call(bf16[6,12,128,128]{3,2,1,0:T(8,128)(2,1)S(1)} %pk_ref.26), custom_call_target="tpu_custom_call" | custom-call | tf_op jit(solution)/shard_map/child_route_cols/cond/branch_2_fun/route_col_2/pallas_call | solution.py:87
  302.1 5.1 copy.186
  332.4 55.0 %conditional.7 = (bf16[13,128,6,128]{3,1,2,0:T(8,128)(2,1)}) conditional(s32[]{:T(128)} %clamp.18, bf16[6,2,128,6,128]{4,3,2,1,0:T(8,128)(2,1)S(1)} %bitcast_dynamic-update-slice_fusion.2, bf16[6,2,128,6,128]{4,3,2,1,0:T(8,128)(2,1)S(1)} %bitcast_dynamic-update-slice_fusion.2, ...), branch_computations={%region_45.48_spmd, %region_46.49_spmd, %region_47.50_spmd, %regio... | conditional | bytes 9633802 | solution.py:103
  332.5 50.5 %route_row_2.3 = bf16[6,2,128,6,128]{4,3,2,1,0:T(8,128)(2,1)} custom-call(bf16[6,2,128,6,128]{4,3,2,1,0:T(8,128)(2,1)S(1)} %pk_ref.42), custom_call_target="tpu_custom_call" | custom-call | tf_op jit(solution)/shard_map/child_route_rows/cond/branch_2_fun/route_row_2/pallas_call | solution.py:87
  382.9 2.5 copy.218
  387.4 3.0 gather_fusion.6
  390.8 2.4 concatenate.62
  393.2 5.2 gather_fusion.5
  398.4 5.2 gather_fusion.7
  403.6 9.6 %fusion = f32[16,128,8,128]{3,1,0,2:T(8,128)} fusion(f32[16,128,8,128]{3,2,1,0:T(8,128)} %param.64, bf16[8,16,128,128]{3,2,1,0:T(8,128)(2,1)} %gather_fusion.7, bf16[8,16,128,128]{3,2,1,0:T(8,128)(2,1)} %gather_fusion.5, pred[8]{0:T(512)(128)(4,1)S(1)} %copy-done.20, pred[8]{0:T(512)(128)(4,1)S(1)} %copy-done.21), kind=kLoop, calls=%fused_computation.18 | loop fusion | flops 12582912 | bytes 25165840 | tf_op jit(solution)/shard_map/assemble/add | solution.py:179
  413.2 9.2 %copy.140 = f32[16,128,8,128]{1,0,3,2:T(8,128)} copy(f32[16,128,8,128]{3,1,0,2:T(8,128)} %fusion) | data formatting | bytes 16777216 | tf_op jit(solution)/shard_map/assemble/add | solution.py:179
  422.4 7.5 copy.242
  429.9 3.2 copy-done.2
  434.5 16.8 %collective-permute-start.1 = (f32[512,128]{0,1:T(8,128)S(1)}, f32[512,128]{0,1:T(8,128)S(1)}, u32[]{:S(2)}, u32[]{:S(2)}) collective-permute-start(f32[512,128]{0,1:T(8,128)S(1)} %get-tuple-element.186), channel_id=1, source_target_pairs={{0,8},{1,9},{2,10},{3,11},{16,24},{17,25},{18,26},{19,27},{32,40},... | collective-permute-start | bytes 786440 | tf_op jit(solution)/shard_map/gather_panel_rows/ppermute | solution.py:113
  452.7 4.8 collective-permute-done.1
  457.5 3.3 collective-permute-done.2
  463.9 4.6 collective-permute-start.4
  468.6 5.3 collective-permute-done.4
  474.8 40.2 %all-gather.7.cloned.1.call-done = f32[8192,128]{0,1:T(8,128)} async-done(((f32[512,128]{0,1:T(8,128)}), f32[8192,128]{0,1:T(8,128)}) %all-gather.7.cloned.1.call-update) | async-done | bytes 4194320 | tf_op jit(solution)/shard_map/gather_panel_rows/all_gather | solution.py:115
  515.0 6.0 reshape.668
  521.0 7.4 copy.141
  528.4 2.6 copy.243
  531.1 4.9 collective-permute-start.3
  536.0 3.8 collective-permute-done.3
  548.9 20.0 %all-gather.9.cloned.1.call-done = f32[512,512]{1,0:T(8,128)} async-done(((f32[64,512]{1,0:T(8,128)}), f32[512,512]{1,0:T(8,128)}) %all-gather.9.cloned.1.call-update) | async-done | bytes 1048592 | tf_op jit(solution)/shard_map/gather_diagonal/all_gather | solution.py:115
  570.4 11.7 %cholesky.130 = f32[128,128]{1,0:T(8,128)S(1)} custom-call(f32[128,128]{1,0:T(8,128)S(1)} %cholesky.194), custom_call_target="Cholesky" | custom-call | tf_op jit(solution)/shard_map/factor_diagonal/jit(cholesky)/cholesky | solution.py:205
  582.2 9.8 %custom-call.21 = f32[1,128,128]{1,2,0:T(8,128)S(1)} custom-call(f32[1,128,128]{2,1,0:T(8,128)S(1)} %get-tuple-element.211), custom_call_target="InvertDiagBlocksLowerTriangular" | custom-call | tf_op jit(solution)/shard_map/factor_diagonal/jit(cholesky)/cholesky | solution.py:205
  592.5 11.7 %cholesky.147 = f32[128,128]{1,0:T(8,128)S(1)} custom-call(f32[128,128]{1,0:T(8,128)S(1)} %convolution_subtract_fusion.6), custom_call_target="Cholesky" | custom-call | tf_op jit(solution)/shard_map/factor_diagonal/jit(cholesky)/cholesky | solution.py:205
  606.9 3.8 while.5
  610.6 19.7 %custom-call.22 = f32[2,128,128]{1,2,0:T(8,128)S(1)} custom-call(f32[2,128,128]{2,1,0:T(8,128)S(1)} %get-tuple-element.139), custom_call_target="InvertDiagBlocksLowerTriangular" | custom-call | tf_op jit(solution)/shard_map/factor_diagonal/triangular_solve/custom-call.0 | solution.py:206
  631.2 3.6 gather_fusion.10
  637.4 2.4 convolution_select_fusion.3
  639.8 4.0 convolution_subtract_fusion.1
  644.4 11.7 %cholesky.164 = f32[128,128]{1,0:T(8,128)S(1)} custom-call(f32[128,128]{1,0:T(8,128)S(1)} %cholesky.197), custom_call_target="Cholesky" | custom-call | tf_op jit(solution)/shard_map/factor_diagonal/jit(cholesky)/cholesky | solution.py:209
  656.2 9.8 %custom-call.23 = f32[1,128,128]{1,2,0:T(8,128)S(1)} custom-call(f32[1,128,128]{2,1,0:T(8,128)S(1)} %get-tuple-element.207), custom_call_target="InvertDiagBlocksLowerTriangular" | custom-call | tf_op jit(solution)/shard_map/factor_diagonal/jit(cholesky)/cholesky | solution.py:209
  666.5 12.1 %cholesky.181 = f32[128,128]{1,0:T(8,128)S(1)} custom-call(f32[128,128]{1,0:T(8,128)S(1)} %convolution_subtract_fusion.5), custom_call_target="Cholesky" | custom-call | tf_op jit(solution)/shard_map/factor_diagonal/jit(cholesky)/cholesky | solution.py:209
  681.4 4.2 while.6
  685.6 19.7 %custom-call.24 = f32[2,128,128]{1,2,0:T(8,128)S(1)} custom-call(f32[2,128,128]{2,1,0:T(8,128)S(1)} %get-tuple-element.140), custom_call_target="InvertDiagBlocksLowerTriangular" | custom-call | tf_op jit(solution)/shard_map/factor_diagonal/triangular_solve/custom-call.0 | solution.py:210
  706.2 4.0 gather_fusion.11
  711.5 8.6 %gather_fusion.9 = f32[2048,256]{1,0:T(8,128)} fusion(f32[256,256]{1,0:T(8,128)S(1)} %get-tuple-element.166, s32[2048]{0:T(1024)S(1)} %get-tuple-element.240), kind=kCustom, calls=%fused_computation.6.clone | custom fusion | bytes 4202496 | tf_op jit(solution)/shard_map/panel_factors/jit(_take)/gather | solution.py:223
  720.1 2.9 copy.149
  723.0 8.6 %gather_fusion.8 = f32[2048,256]{1,0:T(8,128)} fusion(f32[256,256]{1,0:T(8,128)S(1)} %get-tuple-element.168, s32[2048]{0:T(1024)S(1)} %get-tuple-element.239), kind=kCustom, calls=%fused_computation.2.clone | custom fusion | bytes 4202496 | tf_op jit(solution)/shard_map/panel_factors/jit(_take)/gather | solution.py:215
  731.6 2.9 copy.145
  734.6 4.4 convolution_select_fusion.1
  739.1 3.4 convolution_subtract_fusion
  744.1 2.1 convolution_select_fusion
  746.3 16.0 %fusion.2 = f32[2048,1024]{0,1:T(8,128)S(1)} fusion(f32[2048,256]{0,1:T(8,128)S(1)} %convolution_select_fusion, f32[2048,256]{0,1:T(8,128)S(1)} %convolution_select_fusion.1, f32[1024,256]{0,1:T(8,128)S(1)} %convolution_select_fusion.2, f32[1024,256]{0,1:T(8,128)S(1)} %convolution_select_fusion.3, f32[128,8,16,128]{3,2,1,0:T(8,128)S(1)} %bitcast.268), kind=kOutput, calls=%fused_computation.25 | convolution fusion | flops 12888571904 | bytes 23068672 | tf_op jit(solution)/shard_map/trailing_update/dot_general | solution.py:232
  764.3 5.3 copy.232
  769.5 10.7 %copy.157 = f32[16,128,8,128]{3,2,1,0:T(8,128)} copy(f32[16,128,8,128]{1,0,3,2:T(8,128)} %bitcast.269) | data formatting | bytes 16777216 | tf_op jit(solution)/shard_map/reshape | solution.py:238
  (214 shorter events, 95.0 us)
Async XLA Ops:
  6.5 508.5 %all-gather.7.cloned.1.call-start = ((), (), s32[]{:S(2)}) async-start(), calls=%async_computation | async-start | bytes 4456448 | tf_op jit(solution)/shard_map/gather_panel_rows/all_gather | solution.py:115
  42.9 10.4 %copy-start.26 = (s32[12]{0:T(128)S(1)}, s32[12]{0:T(128)}, u32[]{:S(2)}) copy-start(s32[12]{0:T(128)} %iota_add_fusion.1) | copy-start | bytes 148
  42.9 11.1 %copy-start.25 = (s32[6]{0:T(128)S(1)}, s32[6]{0:T(128)}, u32[]{:S(2)}) copy-start(s32[6]{0:T(128)} %iota_add_fusion) | copy-start | bytes 76
  59.5 7.6 copy-start.24
  67.1 7.7 copy-start.9
  232.2 2.4 copy-start.7
  232.3 2.4 copy-start.8
  387.4 3.0 copy-start.22
  390.8 2.4 copy-start.23
  398.4 5.2 copy-start.20
  398.4 5.2 copy-start.21
  429.8 3.3 copy-start.2
  433.2 19.5 %collective-permute-start = (f32[512,128]{0,1:T(8,128)S(1)}, f32[512,128]{0,1:T(8,128)S(1)}, u32[]{:S(2)}, u32[]{:S(2)}) collective-permute-start(f32[512,128]{0,1:T(8,128)S(1)} %get-tuple-element.187), channel_id=1, source_target_pairs={{0,12},{1,13},{2,14},{3,15},{16,28},{17,29},{18,30},{19,31},{32,44... | collective-permute-start | bytes 786440 | tf_op jit(solution)/shard_map/gather_panel_rows/ppermute | solution.py:113
  434.5 23.0 %collective-permute-start.1 = (f32[512,128]{0,1:T(8,128)S(1)}, f32[512,128]{0,1:T(8,128)S(1)}, u32[]{:S(2)}, u32[]{:S(2)}) collective-permute-start(f32[512,128]{0,1:T(8,128)S(1)} %get-tuple-element.186), channel_id=1, source_target_pairs={{0,8},{1,9},{2,10},{3,11},{16,24},{17,25},{18,26},{19,27},{32,40},... | collective-permute-start | bytes 786440 | tf_op jit(solution)/shard_map/gather_panel_rows/ppermute | solution.py:113
  451.3 9.5 %collective-permute-start.2 = (f32[512,128]{0,1:T(8,128)S(1)}, f32[512,128]{0,1:T(8,128)S(1)}, u32[]{:S(2)}, u32[]{:S(2)}) collective-permute-start(f32[512,128]{0,1:T(8,128)S(1)} %get-tuple-element.185), channel_id=1, source_target_pairs={{0,4},{1,5},{2,6},{3,7},{16,20},{17,21},{18,22},{19,23},{32,36},{3... | collective-permute-start | bytes 786440 | tf_op jit(solution)/shard_map/gather_panel_rows/ppermute | solution.py:113
  462.5 82.7 %all-gather.11.cloned.1.call-start = ((), (), s32[]{:S(2)}) async-start(), calls=%async_computation.2 | async-start | bytes 2359296 | tf_op jit(solution)/shard_map/gather_panel_cols/all_gather | solution.py:115
  463.9 10.1 %collective-permute-start.4 = (f32[64,1024]{1,0:T(8,128)S(1)}, f32[64,1024]{1,0:T(8,128)S(1)}, u32[]{:S(2)}, u32[]{:S(2)}) collective-permute-start(f32[64,1024]{1,0:T(8,128)S(1)} %bitcast.305), channel_id=1, source_target_pairs={{0,64},{16,80},{32,96},{48,112},{1,65},{17,81},{33,97},{49,113},{2... | collective-permute-start | bytes 786440 | tf_op jit(solution)/shard_map/gather_panel_cols/ppermute | solution.py:113
  474.7 94.1 %all-gather.9.cloned.1.call-start = ((), (), s32[]{:S(2)}) async-start(), calls=%async_computation.1 | async-start | bytes 1179648 | tf_op jit(solution)/shard_map/gather_diagonal/all_gather | solution.py:115
  531.0 8.8 %copy-start = (f32[256,8,4,128]{3,1,2,0:T(8,128)}, f32[256,8,4,128]{3,1,2,0:T(8,128)S(1)}, u32[]{:S(2)}) copy-start(f32[256,8,4,128]{3,1,2,0:T(8,128)S(1)} %copy.243) | copy-start | bytes 12582916
  531.1 8.7 %collective-permute-start.3 = (f32[64,512]{1,0:T(8,128)S(1)}, f32[64,512]{1,0:T(8,128)S(1)}, u32[]{:S(2)}, u32[]{:S(2)}) collective-permute-start(f32[64,512]{1,0:T(8,128)S(1)} %slice.288), channel_id=1, source_target_pairs={{0,64},{16,80},{32,96},{48,112},{1,65},{17,81},{33,97},{49,113},{2... | collective-permute-start | bytes 393224 | tf_op jit(solution)/shard_map/gather_diagonal/ppermute | solution.py:113
  570.2 36.6 %copy-start.5 = (f32[4,2,64,512]{3,2,1,0:T(8,128)}, f32[4,2,64,512]{3,2,1,0:T(8,128)S(1)}, u32[]{:S(2)}) copy-start(f32[4,2,64,512]{3,2,1,0:T(8,128)S(1)} %copy.142) | copy-start | bytes 3145732
  637.4 6.4 copy-start.10
  731.6 2.9 copy-start.15
  731.6 2.9 copy-start.16
  734.6 4.5 copy-start.1
  739.0 3.6 copy-start.4
  739.0 3.6 copy-start.6
  739.1 3.6 copy-start.17
  739.1 3.6 copy-start.18
  739.1 3.6 copy-start.19
  739.1 7.2 slice-start
  742.5 1.6 copy-start.3
  742.6 1.6 copy-start.12
  742.6 1.6 copy-start.13
  742.6 1.6 copy-start.14
  742.6 3.7 slice-start.1
  762.3 1.1 copy-start.11
Sparse Core Ops, SparseCore 0:
  462.6 52.2 all-gather.6
  516.7 26.4 all-gather.10
  545.0 23.8 all-gather.8

commit v3 on v1

--- a/solution.py
+++ b/solution.py
@@ -1,12 +1,17 @@
+import functools
+
 import jax
 import jax.numpy as jnp
 from jax import lax
+from jax.experimental import pallas as pl
+from jax.experimental.pallas import tpu as pltpu
 from jax.sharding import PartitionSpec as P
 
 PW = 256
 PANELS = 2
 PD = 512
 HI = lax.Precision.HIGHEST
+MESH = pl.DeviceIdType.MESH
 
 
 def decode_map(child_map, lanes):
@@ -23,21 +28,79 @@
     return home, shift, start, inv
 
 
-def routed(packets, axis, devices, start):
-    groups = len(packets)
-
-    def branch(sigma):
-        def run(*pk):
-            return tuple(
-                lax.ppermute(
-                    pk[q], axis, [(j, (sigma + q - j) % devices) for j in range(devices)]
-                )
-                for q in range(groups)
-            )
-
-        return run
-
-    return lax.switch(start % devices, [branch(sg) for sg in range(devices)], *packets)
+def route_kernel(sigma, groups, row_count, col_count, pk_ref, out_ref, send_sem, recv_sem):
+    row_at = lax.axis_index("row")
+    col_at = lax.axis_index("col")
+    sig_r = sigma % row_count
+    targets = []
+    for qr in range(groups):
+        to_row = lax.rem(sig_r + qr - row_at + row_count, row_count)
+        for qc in range(groups):
+            to_col = lax.rem(sigma + qc - col_at + col_count, col_count)
+            mine = (to_row == row_at) & (to_col == col_at)
+            targets.append((qr, qc, to_row, to_col, mine))
+    barrier = pltpu.get_barrier_semaphore()
+    for qr, qc, to_row, to_col, mine in targets:
+
+        @pl.when(jnp.logical_not(mine))
+        def _():
+            pl.semaphore_signal(barrier, 1, device_id=(to_row, to_col), device_id_type=MESH)
+
+    peers = sum(jnp.logical_not(t[4]).astype(jnp.int32) for t in targets)
+    pl.semaphore_wait(barrier, peers)
+
+    copies = []
+    for n, (qr, qc, to_row, to_col, mine) in enumerate(targets):
+        remote = pltpu.make_async_remote_copy(
+            src_ref=pk_ref.at[qr, qc],
+            dst_ref=out_ref.at[qr, qc],
+            send_sem=send_sem.at[n],
+            recv_sem=recv_sem.at[n],
+            device_id=(to_row, to_col),
+            device_id_type=MESH,
+        )
+        local = pltpu.make_async_copy(pk_ref.at[qr, qc], out_ref.at[qr, qc], recv_sem.at[n])
+        copies.append((remote, local, mine))
+
+        @pl.when(jnp.logical_not(mine))
+        def _():
+            remote.start()
+
+        @pl.when(mine)
+        def _():
+            local.start()
+
+    for remote, local, mine in copies:
+
+        @pl.when(jnp.logical_not(mine))
+        def _():
+            remote.wait()
+
+        @pl.when(mine)
+        def _():
+            local.wait()
+
+
+def route_call(packets, sigma, row_count, col_count):
+    groups = packets.shape[0]
+    count = groups * groups
+    return pl.pallas_call(
+        functools.partial(route_kernel, sigma, groups, row_count, col_count),
+        out_shape=jax.ShapeDtypeStruct(packets.shape, packets.dtype),
+        in_specs=[pl.BlockSpec(memory_space=pl.ANY)],
+        out_specs=pl.BlockSpec(memory_space=pl.ANY),
+        scratch_shapes=[pltpu.SemaphoreType.DMA((count,)), pltpu.SemaphoreType.DMA((count,))],
+        compiler_params=pltpu.CompilerParams(collective_id=sigma, has_side_effects=True),
+        name=f"route_{sigma}",
+    )(packets)
+
+
+def routed(packets, start, row_count, col_count):
+    branches = [
+        functools.partial(route_call, sigma=sg, row_count=row_count, col_count=col_count)
+        for sg in range(col_count)
+    ]
+    return lax.switch(start % col_count, branches, packets)
 
 
 def spread_pieces(piece, axis, owners, devices, pieces_axis):
@@ -62,19 +125,13 @@
 
     dense = []
     for i in range(child_count):
-        with jax.named_scope("child_route_cols"):
-            x = child_updates[i].reshape(kr_count, tile, kc_count * tile)
-            col_packets = [
-                lax.dynamic_slice_in_dim(x, inv[i, q] * tile, tile, axis=2) for q in range(groups)
-            ]
-            got = routed(col_packets, "col", col_count, start[i])
-            y = jnp.stack(got, axis=2)
-        with jax.named_scope("child_route_rows"):
-            row_packets = [
-                lax.dynamic_slice_in_dim(y, inv[i, q] * 2, 2, axis=0) for q in range(groups)
-            ]
-            got = routed(row_packets, "row", row_count, start[i])
-            z = jnp.stack(got, axis=0).reshape(groups * 2, tile, groups, tile)
+        with jax.named_scope("child_route"):
+            x = child_updates[i].reshape(groups, kr_count // groups, tile, kc_count, tile)
+            x = jnp.take(x, inv[i], axis=0)
+            x = jnp.take(x, inv[i], axis=3)
+            packets = jnp.transpose(x, (0, 3, 1, 2, 4))
+            got = routed(packets, start[i], row_count, col_count)
+            z = jnp.transpose(got, (0, 2, 3, 1, 4)).reshape(groups * 2, tile, groups, tile)
         with jax.named_scope("child_place"):
             qs = jnp.arange(groups)
             a_of = inv[i]
@@ -138,28 +195,15 @@
         diag = g.reshape(PD, PD)
 
     with jax.named_scope("factor_diagonal"):
-        eye = jnp.eye(PW, dtype=jnp.float32)
-        l11 = jnp.linalg.cholesky(diag[0:PW, 0:PW])
-        w0 = lax.linalg.triangular_solve(l11, eye, left_side=True, lower=True).T
-        l21 = jnp.dot(diag[PW:PD, 0:PW], w0, precision=HI)
-        d22 = diag[PW:PD, PW:PD] - jnp.dot(l21, l21.T, precision=HI)
-        l22 = jnp.linalg.cholesky(d22)
-        w1 = lax.linalg.triangular_solve(l22, eye, left_side=True, lower=True).T
+        factor = jnp.linalg.cholesky(diag)
+        w = lax.linalg.triangular_solve(
+            factor, jnp.eye(PD, dtype=jnp.float32), left_side=True, lower=True
+        ).T
 
     def panel_rows(block, gidx):
-        s0 = jnp.dot(block[:, 0:PW], w0, precision=HI)
-        p0 = jnp.where(
-            (gidx >= PW)[:, None], s0, jnp.take(l11, jnp.clip(gidx, 0, PW - 1), axis=0)
-        )
-        a1 = block[:, PW:PD] - jnp.dot(p0, l21.T, precision=HI)
-        s1 = jnp.dot(a1, w1, precision=HI)
-        in1 = (gidx >= PW) & (gidx < PD)
-        p1 = jnp.where(
-            (gidx >= PD)[:, None],
-            s1,
-            jnp.where(in1[:, None], jnp.take(l22, jnp.clip(gidx - PW, 0, PW - 1), axis=0), 0.0),
-        )
-        return jnp.concatenate([p0, p1], axis=1)
+        solved = jnp.dot(block, w, precision=HI)
+        inside = jnp.take(factor, jnp.clip(gidx, 0, PD - 1), axis=0)
+        return jnp.where((gidx >= PD)[:, None], solved, inside)
 
     with jax.named_scope("panel_factors"):
         pr = panel_rows(g_rows, row_global)

time: 810 us -> 584 us (0.72)
  Pallas kernels: 0 us -> 135 us
  waiting for transfers between devices: 223 us -> 88.5 us
  local copies, waits for them, and re-layouts: 213 us -> 114 us
  starting transfers between devices: 78.1 us -> 11.8 us
  loops' own time: 70.7 us -> 10.9 us
  between operations: 35.8 us -> 20.6 us
  other arithmetic: 137 us -> 148 us
    ppermute x24 -> x0, waiting for transfers between devices: 145 us -> none  [run(): lax.ppermute(pk[q], axis, [(j, (sigma + q - j) % devices) for j in range(...]
    pallas_call x0 -> x2, Pallas kernels: none -> 135 us  [route_call(): pl.pallas_call(functools.partial(route_kernel, sigma, groups, row_count,...]
    ppermute x24 -> x0, starting transfers between devices: 62.9 us -> none  [run(): lax.ppermute(pk[q], axis, [(j, (sigma + q - j) % devices) for j in range(...]
    another operation x6 -> x3, loops' own time: 70.7 us -> 10.9 us  [the longest x2 10.9 us: routed(): return lax.switch(start % col_count, branches, packets)]
    another operation x27 -> x17, local copies, waits for them, and re-layouts: 46.2 us -> 14.4 us  [the longest x2 28.1 us: on_device(): y = jnp.stack(got, axis=2)]
    unnamed x76 -> x24, local copies, waits for them, and re-layouts: 44.1 us -> 15.6 us
    all_gather x3, waiting for transfers between devices: 60.8 us -> 73.5 us  [spread_pieces(): return (lax.all_gather(sub, axis, axis=0, tiled=False), parts, size)]
    reshape x2 -> x1, local copies, waits for them, and re-layouts: 12.5 us -> 0.33 us  [on_device(): diag = g.reshape(PD, PD)]
  transfers between devices with their start and end apart: 32 -> 8, of which waited for: 24 -> 8; matrix products, arithmetic and copies ran while one was open for 5% -> 2% of each run, Pallas kernels for 0% -> 0%
where the time goes in v3:
time: 584 us; the launch traced here: 574 us
  other arithmetic  148 us (25%)
  Pallas kernels  135 us (23%)
  local copies, waits for them, and re-layouts  114 us (20%)
  waiting for transfers between devices  88.5 us (15%)
  matrix products  45.9 us (8%)
  between operations  20.6 us (4%)
  starting transfers between devices  11.8 us (2%)
  loops' own time  10.9 us (2%)
    pallas_call x2, Pallas kernels, route_call(): pl.pallas_call(functools.partial(route_kernel, sigma, groups, row_count,...  135 us
    another operation x15, other arithmetic, on_device(): factor = jnp.linalg.cholesky(diag)  79.5 us
    all_gather x3, waiting for transfers between devices, spread_pieces(): return (lax.all_gather(sub, axis, axis=0, tiled=False), parts, size)  73.5 us
    another operation x3, other arithmetic, on_device(): lax.linalg.triangular_solve(factor, jnp.eye(PD, dtype=jnp.float32), left_...  41.4 us
    dot_general x2, matrix products, panel_rows(): solved = jnp.dot(block, w, precision=HI)  17.9 us
    dot_general x1, matrix products, on_device(): out = a2 - jnp.dot(pr, pc.T, precision=HI)  15.9 us
    unnamed x24, local copies, waits for them, and re-layouts  15.6 us
    ppermute x5, waiting for transfers between devices, spread_pieces(): got = lax.ppermute(part, axis, [(k, m * owners + k) for k in range(owners)])  14.9 us
  transfers between devices with their start and end apart: 8, of which 8 were waited for; matrix products, arithmetic and copies ran while one was open for 2% of the time, Pallas kernels for 0%

profile of v3, /device:TPU:1, one launch (start us, length us, event | category | flops | bytes accessed | tf_op | source)
XLA Modules:
  0.0 574.4 jit_solution(225681374062575130)
XLA Ops:
  15.2 5.2 fusion.98
  20.3 2.3 gather_fusion.6
  22.7 2.0 broadcast_select_fusion.3
  24.6 2.3 gather_fusion.7
  27.0 2.7 gather_fusion.10
  29.7 1.7 broadcast_select_fusion.2
  31.4 4.0 gather_fusion.11
  35.4 2.8 select_bitcast_fusion.1
  38.2 78.7 %conditional.2 = (bf16[6,6,2,128,128]{4,3,2,1,0:T(8,128)(2,1)}) conditional(s32[]{:T(128)} %clamp.26, bf16[6,6,2,128,128]{4,3,2,0,1:T(8,128)(2,1)S(1)} %get-tuple-element.160, bf16[6,6,2,128,128]{4,3,2,0,1:T(8,128)(2,1)S(1)} %get-tuple-element.160, bf16[6,6,2,128,128]{4,3,2,0,1:T(8,128)(2,1)S(1)} %get-tuple-element.160, ...), branch_computations={%region_3.6_spmd, %region_4.7_spmd, %region_5.8_spmd, %region_6.9_... | conditional | bytes 4718600 | solution.py:103
  46.1 1.6 copy.102.pk_ref
  47.7 69.0 %route_8.2 = bf16[6,6,2,128,128]{4,3,2,1,0:T(8,128)(2,1)} custom-call(bf16[6,6,2,128,128]{4,3,2,1,0:T(8,128)(2,1)} %copy.102.pk_ref), custom_call_target="tpu_custom_call" | custom-call | tf_op jit(solution)/shard_map/child_route/cond/branch_8_fun/route_8/pallas_call | solution.py:87
  116.9 3.4 copy.110
  122.1 3.6 concatenate.30
  125.7 4.3 gather_fusion.8
  130.0 2.3 broadcast_select_fusion.1
  132.3 2.4 concatenate.32
  134.9 70.0 %conditional.3 = (bf16[6,6,2,128,128]{4,3,2,1,0:T(8,128)(2,1)S(1)}) conditional(s32[]{:T(128)} %clamp.27, bf16[6,6,2,128,128]{4,3,2,0,1:T(8,128)(2,1)S(1)} %get-tuple-element.159, bf16[6,6,2,128,128]{4,3,2,0,1:T(8,128)(2,1)S(1)} %get-tuple-element.159, ...), branch_computations={%region_21.26_spmd, %region_22.27_spmd, %region_23.28_spmd, %regio... | conditional | bytes 4718600 | solution.py:103
  134.9 1.6 copy.115.pk_ref
  136.5 65.6 %route_2.3 = bf16[6,6,2,128,128]{4,3,2,1,0:T(8,128)(2,1)S(1)} custom-call(bf16[6,6,2,128,128]{4,3,2,1,0:T(8,128)(2,1)} %copy.115.pk_ref), custom_call_target="tpu_custom_call" | custom-call | tf_op jit(solution)/shard_map/child_route/cond/branch_2_fun/route_2/pallas_call | solution.py:87
  205.3 2.6 gather_fusion.12
  207.9 2.2 broadcast_select_fusion
  210.2 2.4 concatenate.35
  212.6 5.1 gather_fusion.9
  217.6 5.1 gather_fusion.13
  222.8 8.0 %fusion = f32[16,128,8,128]{3,1,0,2:T(8,128)S(1)} fusion(f32[16,128,8,128]{3,2,1,0:T(8,128)} %param.45, bf16[8,16,128,128]{3,2,1,0:T(8,128)(2,1)} %gather_fusion.13, bf16[8,16,128,128]{3,2,1,0:T(8,128)(2,1)} %gather_fusion.9, pred[8]{0:T(512)(128)(4,1)S(1)} %get-tuple-element.111, pred[8]{0:T(512)(128)(4,1)S(1)} %get-tuple-element.155), kind=kLoop, calls=%fused_computation.18 | loop fusion | flops 12582912 | bytes 25165840 | tf_op jit(solution)/shard_map/assemble/add | solution.py:173
  230.8 6.6 %copy.130 = f32[16,128,8,128]{3,2,1,0:T(8,128)S(1)} copy(f32[16,128,8,128]{3,1,0,2:T(8,128)S(1)} %fusion) | data formatting | bytes 16777216 | tf_op jit(solution)/shard_map/assemble/add | solution.py:173
  237.4 2.2 copy.152
  239.6 1.5 copy-done
  241.2 3.4 copy-done.4
  246.0 1.4 collective-permute-start.1
  249.3 3.1 collective-permute-done.1
  252.4 2.8 collective-permute-done.2
  255.2 1.7 fusion.21
  258.3 3.1 collective-permute-start.4
  261.5 2.9 collective-permute-done.4
  265.3 43.2 %all-gather.7.cloned.1.call-done = f32[8192,128]{1,0:T(8,128)} async-done(((f32[512,128]{1,0:T(8,128)}), f32[8192,128]{1,0:T(8,128)}) %all-gather.7.cloned.1.call-update) | async-done | bytes 4194320 | tf_op jit(solution)/shard_map/gather_panel_rows/all_gather | solution.py:115
  308.5 4.9 copy.131
  313.9 1.5 copy-done.1
  315.3 4.6 collective-permute-start.3
  320.0 5.5 collective-permute-done.3
  327.3 9.4 %all-gather.11.cloned.1.call-done = f32[512,1024]{1,0:T(8,128)} async-done(((f32[64,1024]{1,0:T(8,128)}), f32[512,1024]{1,0:T(8,128)}) %all-gather.11.cloned.1.call-update) | async-done | bytes 2097168 | tf_op jit(solution)/shard_map/gather_panel_cols/all_gather | solution.py:115
  336.7 3.2 copy.136
  339.9 20.9 %all-gather.9.cloned.1.call-done = f32[512,512]{1,0:T(8,128)} async-done(((f32[64,512]{1,0:T(8,128)}), f32[512,512]{1,0:T(8,128)}) %all-gather.9.cloned.1.call-update) | async-done | bytes 1048592 | tf_op jit(solution)/shard_map/gather_diagonal/all_gather | solution.py:115
  363.7 11.7 %cholesky.104 = f32[128,128]{1,0:T(8,128)S(1)} custom-call(f32[128,128]{1,0:T(8,128)S(1)} %cholesky.266), custom_call_target="Cholesky" | custom-call | tf_op jit(solution)/shard_map/factor_diagonal/jit(cholesky)/cholesky | solution.py:198
  375.5 9.8 %custom-call.30 = f32[1,128,128]{1,2,0:T(8,128)S(1)} custom-call(f32[1,128,128]{2,1,0:T(8,128)S(1)} %get-tuple-element.141), custom_call_target="InvertDiagBlocksLowerTriangular" | custom-call | tf_op jit(solution)/shard_map/factor_diagonal/jit(cholesky)/cholesky | solution.py:198
  387.9 11.7 %cholesky.217 = f32[128,128]{1,0:T(8,128)S(1)} custom-call(f32[128,128]{1,0:T(8,128)S(1)} %cholesky.270), custom_call_target="Cholesky" | custom-call | tf_op jit(solution)/shard_map/factor_diagonal/jit(cholesky)/cholesky | solution.py:198
  401.0 10.2 %custom-call.31 = f32[1,128,128]{1,2,0:T(8,128)S(1)} custom-call(f32[1,128,128]{2,1,0:T(8,128)S(1)} %get-tuple-element.138), custom_call_target="InvertDiagBlocksLowerTriangular" | custom-call | tf_op jit(solution)/shard_map/factor_diagonal/jit(cholesky)/cholesky | solution.py:198
  412.8 11.7 %cholesky.238 = f32[128,128]{1,0:T(8,128)S(1)} custom-call(f32[128,128]{1,0:T(8,128)S(1)} %cholesky.275), custom_call_target="Cholesky" | custom-call | tf_op jit(solution)/shard_map/factor_diagonal/jit(cholesky)/cholesky | solution.py:198
  425.1 9.8 %custom-call.32 = f32[1,128,128]{1,2,0:T(8,128)S(1)} custom-call(f32[1,128,128]{2,1,0:T(8,128)S(1)} %get-tuple-element.135), custom_call_target="InvertDiagBlocksLowerTriangular" | custom-call | tf_op jit(solution)/shard_map/factor_diagonal/jit(cholesky)/cholesky | solution.py:198
  436.4 11.8 %cholesky.255 = f32[128,128]{1,0:T(8,128)S(1)} custom-call(f32[128,128]{1,0:T(8,128)S(1)} %convolution_subtract_fusion.6), custom_call_target="Cholesky" | custom-call | tf_op jit(solution)/shard_map/factor_diagonal/jit(cholesky)/cholesky | solution.py:198
  452.6 14.2 %while.2 = (s32[]{:T(128)}, f32[512,512]{1,0:T(8,128)}, s32[4,2]{0,1:T(2,128)S(1)}, f32[4,128,128]{2,1,0:T(8,128)}, s32[]{:T(128)}) while((s32[]{:T(128)}, f32[512,512]{1,0:T(8,128)}, s32[4,2]{0,1:T(2,128)S(1)}, f32[4,128,128]{2,1,0:T(8,128)}, s32[]{:T(128)}) %tuple.158), condition=%wide.while_cond.1, body=%wide.while_body.1.sunk | while | flops 2 | bytes 132705 | solution.py:199
  453.3 2.9 bitcast_dynamic-update-slice_fusion.2
  456.8 2.9 bitcast_dynamic-update-slice_fusion.2
  460.4 2.9 bitcast_dynamic-update-slice_fusion.2
  464.0 2.9 bitcast_dynamic-update-slice_fusion.2
  466.9 40.1 %custom-call.33 = f32[4,128,128]{1,2,0:T(8,128)S(1)} custom-call(f32[4,128,128]{2,1,0:T(8,128)} %get-tuple-element.94), custom_call_target="InvertDiagBlocksLowerTriangular" | custom-call | tf_op jit(solution)/shard_map/factor_diagonal/triangular_solve | solution.py:199
  509.0 1.4 convolution_subtract_fusion.1
  510.8 1.7 convolution_subtract_fusion.3
  513.7 8.9 %gather_fusion.4 = f32[2048,512]{1,0:T(8,128)} fusion(f32[512,512]{1,0:T(8,128)S(1)} %get-tuple-element.108, s32[2048]{0:T(1024)S(1)} %broadcast_clamp_fusion), kind=kCustom, calls=%fused_computation.12 | custom fusion | bytes 8396800 | tf_op jit(solution)/shard_map/panel_factors/jit(_take)/gather | solution.py:205
  522.6 3.5 gather_fusion.5
  526.1 8.6 %fusion.14 = f32[1024,512]{1,0:T(8,128)S(1)} fusion(f32[512,1024]{1,0:T(8,128)} %bitcast.164, f32[128,512]{1,0:T(8,128)} %fusion.31, f32[128,512]{1,0:T(8,128)} %copy-done.6, f32[128,512]{1,0:T(8,128)} %copy-done.5, f32[128,512]{1,0:T(8,128)S(1)} %fusion.22), kind=kOutput, calls=%fused_computation.56 | convolution fusion | flops 3222011904 | bytes 5242880 | tf_op jit(solution)/shard_map/panel_factors/dot_general | solution.py:204
  534.7 9.4 %select_select_fusion = f32[2048,512]{1,0:T(8,128)S(1)} fusion(f32[2048,512]{1,0:T(8,128)} %gather_fusion.4, pred[2048]{0:T(1024)(128)(4,1)S(1)} %get-tuple-element.161, pred[2048]{0:T(1024)(128)(4,1)S(1)} %get-tuple-element.162, f32[128,512]{1,0:T(8,128)} %fusion.31, f32[128,512]{1,0:T(8,128)} %copy-done.6, f32[128,512]{1,0:T(8,128)} %copy-done.5, ...), kind=kOutput, calls=%fused_computation.21 | convolution fusion | flops 6445334528 | bytes 13635584 | tf_op jit(solution)/shard_map/panel_factors/dot_general | solution.py:204
  544.1 15.9 %convolution_subtract_fusion = f32[2048,1024]{1,0:T(8,128)S(1)} fusion(f32[2048,512]{1,0:T(8,128)S(1)} %select_select_fusion, f32[1024,512]{1,0:T(8,128)S(1)} %fusion.14, f32[1024,512]{1,0:T(8,128)S(1)} %gather_fusion.5, pred[1024]{0:T(1024)(128)(4,1)S(1)} %get-tuple-element.163, pred[1024]{0:T(1024)(128)(4,1)S(1)} %get-tuple-element.164, ...), kind=kOutput, calls=%fused_computation.22 | convolution fusion | flops 12888047616 | bytes 25167872 | tf_op jit(solution)/shard_map/trailing_update/dot_general | solution.py:213
  562.0 5.5 copy.141
  (122 shorter events, 35.5 us)
Async XLA Ops:
  6.5 302.0 %all-gather.7.cloned.1.call-start = ((), (), s32[]{:S(2)}) async-start(), calls=%async_computation | async-start | bytes 4456448 | tf_op jit(solution)/shard_map/gather_panel_rows/all_gather | solution.py:115
  230.8 6.6 %copy-start.3 = (f32[16,128,8,128]{3,1,0,2:T(8,128)}, f32[16,128,8,128]{3,1,0,2:T(8,128)S(1)}, u32[]{:S(2)}) copy-start(f32[16,128,8,128]{3,1,0,2:T(8,128)S(1)} %fusion) | copy-start | bytes 25165828
  237.4 3.7 copy-start
  241.2 3.4 copy-start.4
  244.7 4.6 collective-permute-start
  246.0 6.4 %collective-permute-start.1 = (f32[512,128]{1,0:T(8,128)S(1)}, f32[512,128]{1,0:T(8,128)S(1)}, u32[]{:S(2)}, u32[]{:S(2)}) collective-permute-start(f32[512,128]{1,0:T(8,128)S(1)} %get-tuple-element.128), channel_id=1, source_target_pairs={{0,8},{1,9},{2,10},{3,11},{16,24},{17,25},{18,26},{19,27},{32,40},... | collective-permute-start | bytes 786440 | tf_op jit(solution)/shard_map/gather_panel_rows/ppermute | solution.py:113
  247.4 7.8 %collective-permute-start.2 = (f32[512,128]{1,0:T(8,128)S(1)}, f32[512,128]{1,0:T(8,128)S(1)}, u32[]{:S(2)}, u32[]{:S(2)}) collective-permute-start(f32[512,128]{1,0:T(8,128)S(1)} %get-tuple-element.127), channel_id=1, source_target_pairs={{0,4},{1,5},{2,6},{3,7},{16,20},{17,21},{18,22},{19,23},{32,36},{3... | collective-permute-start | bytes 786440 | tf_op jit(solution)/shard_map/gather_panel_rows/ppermute | solution.py:113
  256.9 79.8 %all-gather.11.cloned.1.call-start = ((), (), s32[]{:S(2)}) async-start(), calls=%async_computation.2 | async-start | bytes 2359296 | tf_op jit(solution)/shard_map/gather_panel_cols/all_gather | solution.py:115
  258.3 6.2 %collective-permute-start.4 = (f32[64,1024]{1,0:T(8,128)S(1)}, f32[64,1024]{1,0:T(8,128)S(1)}, u32[]{:S(2)}, u32[]{:S(2)}) collective-permute-start(f32[64,1024]{1,0:T(8,128)S(1)} %bitcast.172), channel_id=1, source_target_pairs={{0,64},{16,80},{32,96},{48,112},{1,65},{17,81},{33,97},{49,113},{2... | collective-permute-start | bytes 786440 | tf_op jit(solution)/shard_map/gather_panel_cols/ppermute | solution.py:113
  265.2 95.6 %all-gather.9.cloned.1.call-start = ((), (), s32[]{:S(2)}) async-start(), calls=%async_computation.1 | async-start | bytes 1179648 | tf_op jit(solution)/shard_map/gather_diagonal/all_gather | solution.py:115
  313.4 1.9 copy-start.1
  315.3 10.2 %collective-permute-start.3 = (f32[64,512]{1,0:T(8,128)S(1)}, f32[64,512]{1,0:T(8,128)S(1)}, u32[]{:S(2)}, u32[]{:S(2)}) collective-permute-start(f32[64,512]{1,0:T(8,128)S(1)} %slice.253), channel_id=1, source_target_pairs={{0,64},{16,80},{32,96},{48,112},{1,65},{17,81},{33,97},{49,113},{2... | collective-permute-start | bytes 393224 | tf_op jit(solution)/shard_map/gather_diagonal/ppermute | solution.py:113
  362.7 1.0 copy-start.7
  508.9 1.9 copy-start.5
  510.8 1.7 copy-start.6
  526.1 8.6 %copy-start.2 = (f32[4,4,512,128]{3,1,2,0:T(4,128)S(1)}, f32[4,4,512,128]{3,1,2,0:T(4,128)}, u32[]{:S(2)}) copy-start(f32[4,4,512,128]{3,1,2,0:T(4,128)} %copy-done.1) | copy-start | bytes 12582916
  526.1 18.0 %slice-start = ((s8[8388608]{0:T(1024)(128)(4,1)}), s8[4194304]{0:T(1024)(128)(4,1)S(1)}, s32[]{:S(2)}) async-start(s8[8388608]{0:T(1024)(128)(4,1)} %bitcast.152), calls=%async_computation.3 | async-start | bytes 8388608
  534.7 9.4 %slice-start.1 = ((s8[8388608]{0:T(1024)(128)(4,1)}), s8[4194304]{0:T(1024)(128)(4,1)S(1)}, s32[]{:S(2)}) async-start(s8[8388608]{0:T(1024)(128)(4,1)} %bitcast.152), calls=%async_computation.4 | async-start | bytes 8388608
Sparse Core Ops, SparseCore 0:
  257.0 51.4 all-gather.6
  310.2 26.4 all-gather.10
  338.4 22.2 all-gather.8

commit v4 on v3

--- a/solution.py
+++ b/solution.py
@@ -181,6 +181,13 @@
     col_global = (local_cols // tile * col_count + col_index) * tile + local_cols % tile
     owners = PD // tile
 
+    with jax.named_scope("gather_diagonal"):
+        g, parts, size = spread_pieces(a2[0:tile, 0:tile], "col", owners, col_count, 0)
+        g = g.reshape(parts, owners, size, tile).transpose(0, 2, 1, 3)
+        strip = g.reshape(tile, PD)
+        g, parts, size = spread_pieces(strip, "row", owners, row_count, 0)
+        g = g.reshape(parts, owners, size, PD).transpose(1, 0, 2, 3)
+        diag = g.reshape(PD, PD)
     with jax.named_scope("gather_panel_rows"):
         g, parts, size = spread_pieces(a2[:, 0:tile], "col", owners, col_count, 0)
         g = g.reshape(parts, owners, size, tile).transpose(0, 2, 1, 3)
@@ -189,10 +196,6 @@
         g, parts, size = spread_pieces(a2[0:tile, :], "row", owners, row_count, 0)
         g = g.reshape(parts, owners, size, breadth).transpose(1, 0, 2, 3)
         g_cols = g.reshape(PD, breadth)
-    with jax.named_scope("gather_diagonal"):
-        g, parts, size = spread_pieces(g_rows[0:tile, :], "row", owners, row_count, 0)
-        g = g.reshape(parts, owners, size, PD).transpose(1, 0, 2, 3)
-        diag = g.reshape(PD, PD)
 
     with jax.named_scope("factor_diagonal"):
         factor = jnp.linalg.cholesky(diag)
@@ -200,22 +203,24 @@
             factor, jnp.eye(PD, dtype=jnp.float32), left_side=True, lower=True
         ).T
 
-    def panel_rows(block, gidx):
+    def panel_rows(block, at):
         solved = jnp.dot(block, w, precision=HI)
-        inside = jnp.take(factor, jnp.clip(gidx, 0, PD - 1), axis=0)
-        return jnp.where((gidx >= PD)[:, None], solved, inside)
+        inside = lax.dynamic_slice_in_dim(factor, jnp.minimum(at, owners - 1) * tile, tile, axis=0)
+        head = jnp.where(at < owners, inside, solved[0:tile])
+        return lax.dynamic_update_slice_in_dim(solved, head, 0, axis=0)
 
     with jax.named_scope("panel_factors"):
-        pr = panel_rows(g_rows, row_global)
-        pc = panel_rows(g_cols.T, col_global)
+        pr = panel_rows(g_rows, row_index)
+        pc = panel_rows(g_cols.T, col_index)
 
     with jax.named_scope("trailing_update"):
         out = a2 - jnp.dot(pr, pc.T, precision=HI)
         own = lax.dynamic_slice_in_dim(pr, jnp.minimum(col_index, owners - 1) * tile, tile, axis=1)
         first = jnp.where(col_index < owners, own, out[:, 0:tile])
-        out = out.at[:, 0:tile].set(first)
-        upper = (row_global[:, None] < PD) & (col_global[None, :] >= PD)
-        out = jnp.where(upper, 0.0, out)
+        out = lax.dynamic_update_slice_in_dim(out, first, 0, axis=1)
+        top = out[0:tile]
+        top = jnp.where((row_index < owners) & (col_global >= PD)[None, :], 0.0, top)
+        out = lax.dynamic_update_slice_in_dim(out, top, 0, axis=0)
     return out.reshape(slots_r, tile, slots_c, tile)
 
 

time: 584 us -> 528 us (0.904)
  the two profiles are of different devices: /device:TPU:1 before, /device:TPU:20 now
where the time goes in v4:
time: 528 us; the launch traced here: 518 us
  other arithmetic  147 us (28%)
  Pallas kernels  127 us (24%)
  local copies, waits for them, and re-layouts  92.5 us (18%)
  matrix products  41.9 us (8%)
  waiting for transfers between devices  37.3 us (7%)
  blocking collectives  23.1 us (4%)
  between operations  20.6 us (4%)
  loops' own time  20.3 us (4%)
  starting transfers between devices  8.33 us (2%)
    pallas_call x2, Pallas kernels, route_call(): pl.pallas_call(functools.partial(route_kernel, sigma, groups, row_count,...  127 us
    another operation x15, other arithmetic, on_device(): factor = jnp.linalg.cholesky(diag)  79.5 us
    another operation x3, other arithmetic, on_device(): lax.linalg.triangular_solve(factor, jnp.eye(PD, dtype=jnp.float32), left_...  41.4 us
    ppermute x8, waiting for transfers between devices, spread_pieces(): got = lax.ppermute(part, axis, [(k, m * owners + k) for k in range(owners)])  37.2 us
    all_gather x1, blocking collectives, spread_pieces(): return (lax.all_gather(sub, axis, axis=0, tiled=False), parts, size)  23.1 us
    another operation x2, loops' own time, routed(): return lax.switch(start % col_count, branches, packets)  20.3 us
    dot_general x1, matrix products, on_device(): out = a2 - jnp.dot(pr, pc.T, precision=HI)  16.3 us
    dot_general x2, matrix products, panel_rows(): solved = jnp.dot(block, w, precision=HI)  14.5 us
  transfers between devices with their start and end apart: 11, of which 4 were waited for; matrix products, arithmetic and copies ran while one was open for 31% of the time, Pallas kernels for 0%

profile of v4, /device:TPU:20, one launch (start us, length us, event | category | flops | bytes accessed | tf_op | source)
XLA Modules:
  0.0 518.0 jit_solution(16248658258418040062)
XLA Ops:
  17.3 5.2 %fusion.82 = (bf16[1,12,128,6,128]{4,2,3,1,0:T(8,128)(2,1)S(1)}, bf16[1,12,128,6,128]{4,2,3,1,0:T(8,128)(2,1)}) fusion(bf16[2,12,128,6,128]{4,2,3,1,0:T(8,128)(2,1)} %param.44), kind=kLoop, calls=%fused_computation.231 | loop fusion | bytes 9437184 | tf_op jit(solution)/shard_map/child_route/slice | solution.py:129
  22.5 2.3 gather_fusion.4
  24.8 2.0 broadcast_select_fusion.3
  26.8 2.3 gather_fusion.5
  29.1 2.7 gather_fusion.8
  31.8 1.7 broadcast_select_fusion.2
  33.5 4.0 gather_fusion.9
  37.5 2.8 select_bitcast_fusion
  40.3 69.5 %conditional.3 = (bf16[6,6,2,128,128]{4,3,2,1,0:T(8,128)(2,1)}) conditional(s32[]{:T(128)} %clamp.7, bf16[6,6,2,128,128]{4,3,2,0,1:T(8,128)(2,1)S(1)} %get-tuple-element.154, bf16[6,6,2,128,128]{4,3,2,0,1:T(8,128)(2,1)S(1)} %get-tuple-element.154, bf16[6,6,2,128,128]{4,3,2,0,1:T(8,128)(2,1)S(1)} %get-tuple-element.154, ...), branch_computations={%region_21.26_spmd, %region_22.27_spmd, %region_23.28_spmd, %regio... | conditional | bytes 4718600 | solution.py:103
  49.2 1.6 copy.129.pk_ref
  50.8 59.1 %route_14.3 = bf16[6,6,2,128,128]{4,3,2,1,0:T(8,128)(2,1)} custom-call(bf16[6,6,2,128,128]{4,3,2,1,0:T(8,128)(2,1)} %copy.129.pk_ref), custom_call_target="tpu_custom_call" | custom-call | tf_op jit(solution)/shard_map/child_route/cond/branch_14_fun/route_14/pallas_call | solution.py:87
  109.9 1.9 copy.131
  111.8 1.8 concatenate.31
  113.6 4.3 gather_fusion.10
  117.9 2.3 broadcast_select_fusion
  120.2 2.3 concatenate.33
  122.6 80.6 %conditional.2 = (bf16[6,6,2,128,128]{4,3,2,1,0:T(8,128)(2,1)S(1)}) conditional(s32[]{:T(128)} %clamp.6, bf16[6,6,2,128,128]{4,3,2,0,1:T(8,128)(2,1)S(1)} %get-tuple-element.155, bf16[6,6,2,128,128]{4,3,2,0,1:T(8,128)(2,1)S(1)} %get-tuple-element.155, ...), branch_computations={%region_3.6_spmd, %region_4.7_spmd, %region_5.8_spmd, %region_6.9_... | conditional | bytes 4718600 | solution.py:103
  122.8 1.6 copy.103.pk_ref
  124.3 67.7 %route_7.2 = bf16[6,6,2,128,128]{4,3,2,1,0:T(8,128)(2,1)S(1)} custom-call(bf16[6,6,2,128,128]{4,3,2,1,0:T(8,128)(2,1)} %copy.103.pk_ref), custom_call_target="tpu_custom_call" | custom-call | tf_op jit(solution)/shard_map/child_route/cond/branch_7_fun/route_7/pallas_call | solution.py:87
  203.6 2.6 gather_fusion.6
  206.2 2.3 broadcast_select_fusion.1
  208.5 2.4 concatenate.30
  210.9 5.1 gather_fusion.11
  216.0 5.1 gather_fusion.7
  221.1 7.6 %fusion = f32[16,128,8,128]{3,1,0,2:T(8,128)S(1)} fusion(f32[16,128,8,128]{3,2,1,0:T(8,128)} %param.43, bf16[8,16,128,128]{3,2,1,0:T(8,128)(2,1)} %gather_fusion.11, bf16[8,16,128,128]{3,2,1,0:T(8,128)(2,1)} %gather_fusion.7, pred[8]{0:T(512)(128)(4,1)S(1)} %get-tuple-element.99, pred[8]{0:T(512)(128)(4,1)S(1)} %get-tuple-element.150), kind=kLoop, calls=%fused_computation.16 | loop fusion | flops 12582912 | bytes 25165840 | tf_op jit(solution)/shard_map/assemble/add | solution.py:173
  228.7 6.6 %copy.132 = f32[16,128,8,128]{3,2,1,0:T(8,128)S(1)} copy(f32[16,128,8,128]{3,1,0,2:T(8,128)S(1)} %fusion) | data formatting | bytes 16777216 | tf_op jit(solution)/shard_map/assemble/add | solution.py:173
  235.3 2.2 copy.162
  237.5 1.5 copy-done
  239.0 3.2 copy-done.2
  242.9 1.3 collective-permute-start.4
  244.9 5.1 collective-permute-done.4
  250.8 23.1 %all-gather.1 = f32[512,128]{1,0:T(8,128)S(1)} all-gather(f32[32,128]{1,0:T(8,128)S(1)} %fusion.42), channel_id=3, replica_groups=mesh['row'=8,'col'=16] {'col'}, dimensions={0}, use_global_device_ids=true | all-gather | bytes 278528 | tf_op jit(solution)/shard_map/gather_diagonal/all_gather | solution.py:115
  274.2 1.3 collective-permute-start.6
  275.5 7.0 %collective-permute-done.6 = f32[64,512]{1,0:T(8,128)S(1)} collective-permute-done((f32[64,512]{1,0:T(8,128)S(1)}, f32[64,512]{1,0:T(8,128)S(1)}, u32[]{:S(2)}, u32[]{:S(2)}) %collective-permute-start.6) | collective-permute-done | bytes 131104 | tf_op jit(solution)/shard_map/gather_diagonal/ppermute | solution.py:113
  284.6 1.3 collective-permute-start.7
  286.0 10.6 %collective-permute-done.7 = f32[64,1024]{1,0:T(8,128)S(1)} collective-permute-done((f32[64,1024]{1,0:T(8,128)S(1)}, f32[64,1024]{1,0:T(8,128)S(1)}, u32[]{:S(2)}, u32[]{:S(2)}) %collective-permute-start.7) | collective-permute-done | bytes 262176 | tf_op jit(solution)/shard_map/gather_panel_cols/ppermute | solution.py:113
  299.3 1.3 collective-permute-start.1
  301.7 14.4 %collective-permute-done.1 = f32[512,128]{1,0:T(8,128)S(1)} collective-permute-done((f32[512,128]{1,0:T(8,128)S(1)}, f32[512,128]{1,0:T(8,128)S(1)}, u32[]{:S(2)}, u32[]{:S(2)}) %collective-permute-start.1) | collective-permute-done | bytes 262176 | tf_op jit(solution)/shard_map/gather_panel_rows/ppermute | solution.py:113
  316.2 1.7 fusion.22
  318.9 1.7 copy.135
  322.2 11.7 %cholesky.104 = f32[128,128]{1,0:T(8,128)S(1)} custom-call(f32[128,128]{1,0:T(8,128)S(1)} %cholesky.266), custom_call_target="Cholesky" | custom-call | tf_op jit(solution)/shard_map/factor_diagonal/jit(cholesky)/cholesky | solution.py:201
  333.9 9.8 %custom-call.30 = f32[1,128,128]{1,2,0:T(8,128)S(1)} custom-call(f32[1,128,128]{2,1,0:T(8,128)S(1)} %get-tuple-element.136), custom_call_target="InvertDiagBlocksLowerTriangular" | custom-call | tf_op jit(solution)/shard_map/factor_diagonal/jit(cholesky)/cholesky | solution.py:201
  343.9 1.2 constant_dynamic-update-slice_fusion
  345.1 1.3 convolution_subtract_fusion.4
  346.4 11.7 %cholesky.217 = f32[128,128]{1,0:T(8,128)S(1)} custom-call(f32[128,128]{1,0:T(8,128)S(1)} %cholesky.270), custom_call_target="Cholesky" | custom-call | tf_op jit(solution)/shard_map/factor_diagonal/jit(cholesky)/cholesky | solution.py:201
  358.2 10.0 %custom-call.31 = f32[1,128,128]{1,2,0:T(8,128)S(1)} custom-call(f32[1,128,128]{2,1,0:T(8,128)S(1)} %get-tuple-element.133), custom_call_target="InvertDiagBlocksLowerTriangular" | custom-call | tf_op jit(solution)/shard_map/factor_diagonal/jit(cholesky)/cholesky | solution.py:201
  368.4 1.3 convolution_subtract_fusion.5
  369.7 11.7 %cholesky.238 = f32[128,128]{1,0:T(8,128)S(1)} custom-call(f32[128,128]{1,0:T(8,128)S(1)} %cholesky.275), custom_call_target="Cholesky" | custom-call | tf_op jit(solution)/shard_map/factor_diagonal/jit(cholesky)/cholesky | solution.py:201
  381.4 9.8 %custom-call.32 = f32[1,128,128]{1,2,0:T(8,128)S(1)} custom-call(f32[1,128,128]{2,1,0:T(8,128)S(1)} %get-tuple-element.130), custom_call_target="InvertDiagBlocksLowerTriangular" | custom-call | tf_op jit(solution)/shard_map/factor_diagonal/jit(cholesky)/cholesky | solution.py:201
  392.7 12.1 %cholesky.255 = f32[128,128]{1,0:T(8,128)S(1)} custom-call(f32[128,128]{1,0:T(8,128)S(1)} %convolution_subtract_fusion.6), custom_call_target="Cholesky" | custom-call | tf_op jit(solution)/shard_map/factor_diagonal/jit(cholesky)/cholesky | solution.py:201
  411.1 10.6 %while.1 = (s32[]{:T(128)}, f32[512,512]{1,0:T(8,128)S(1)}, s32[4,2]{0,1:T(2,128)S(1)}, f32[4,128,128]{2,1,0:T(8,128)}, s32[]{:T(128)}) while((s32[]{:T(128)}, f32[512,512]{1,0:T(8,128)S(1)}, s32[4,2]{0,1:T(2,128)S(1)}, f32[4,128,128]{2,1,0:T(8,128)}, s32[]{:T(128)}) %tuple.156), condition=%wide.while_cond, body=%wide.while_body.sunk | while | flops 2 | bytes 132205 | solution.py:202
  411.8 2.0 bitcast_dynamic-update-slice_fusion.2
  414.5 2.0 bitcast_dynamic-update-slice_fusion.2
  417.1 2.0 bitcast_dynamic-update-slice_fusion.2
  419.7 2.0 bitcast_dynamic-update-slice_fusion.2
  421.7 40.1 %custom-call.33 = f32[4,128,128]{1,2,0:T(8,128)S(1)} custom-call(f32[4,128,128]{2,1,0:T(8,128)} %get-tuple-element.82), custom_call_target="InvertDiagBlocksLowerTriangular" | custom-call | tf_op jit(solution)/shard_map/factor_diagonal/triangular_solve | solution.py:202
  463.8 1.4 convolution_subtract_fusion.1
  465.6 1.6 convolution_subtract_fusion.3
  467.6 1.7 copy.139
  469.3 6.9 %fusion.12 = f32[1024,512]{1,0:T(8,128)S(1)} fusion(f32[512,1024]{1,0:T(8,128)S(1)} %bitcast.176, f32[128,512]{1,0:T(8,128)S(1)} %fusion.32, f32[128,512]{1,0:T(8,128)S(1)} %fusion.33, f32[128,512]{1,0:T(8,128)S(1)} %fusion.35, f32[128,512]{1,0:T(8,128)S(1)} %fusion.23), kind=kOutput, calls=%fused_computation.49 | convolution fusion | flops 3222011904 | bytes 5242880 | tf_op jit(solution)/shard_map/panel_factors/dot_general | solution.py:207
  476.2 4.9 copy.133
  481.2 7.6 %fusion.1 = f32[2048,512]{1,0:T(8,128)S(1)} fusion(f32[256,8,4,128]{3,2,1,0:T(4,128)S(1)} %bitcast.166, f32[128,512]{1,0:T(8,128)S(1)} %fusion.32, f32[128,512]{1,0:T(8,128)S(1)} %fusion.33, f32[128,512]{1,0:T(8,128)S(1)} %fusion.35, f32[128,512]{1,0:T(8,128)S(1)} %fusion.23), kind=kOutput, calls=%fused_computation.17 | convolution fusion | flops 6443237376 | bytes 9437184 | tf_op jit(solution)/shard_map/panel_factors/dot_general | solution.py:207
  489.0 16.3 %convolution_subtract_fusion = f32[2048,1024]{1,0:T(8,128)S(1)} fusion(f32[2048,512]{1,0:T(8,128)S(1)} %get-tuple-element.124, f32[1024,512]{1,0:T(8,128)S(1)} %get-tuple-element.123, f32[256,8,8,128]{3,2,1,0:T(8,128)S(1)} %bitcast.164), kind=kOutput, calls=%fused_computation.20 | convolution fusion | flops 12886999040 | bytes 23068672 | tf_op jit(solution)/shard_map/trailing_update/dot_general | solution.py:217
  505.6 5.5 %copy.146 = f32[256,8,8,128]{3,2,1,0:T(8,128)} copy(f32[256,8,8,128]{3,1,2,0:T(8,128)S(1)} %bitcast.165) | data formatting | bytes 16777216
  (120 shorter events, 29.7 us)
Async XLA Ops:
  6.5 312.4 %all-gather.10.cloned.1.call-start = ((), (), s32[]{:S(2)}) async-start(), calls=%async_computation.1 | async-start | bytes 1179648 | tf_op jit(solution)/shard_map/gather_diagonal/all_gather | solution.py:115
  228.6 6.6 %copy-start.1 = (f32[16,128,8,128]{3,1,0,2:T(8,128)}, f32[16,128,8,128]{3,1,0,2:T(8,128)S(1)}, u32[]{:S(2)}) copy-start(f32[16,128,8,128]{3,1,0,2:T(8,128)S(1)} %fusion) | copy-start | bytes 25165828
  235.3 3.7 copy-start
  239.0 3.2 copy-start.2
  242.3 2.7 collective-permute-start.5
  242.9 7.1 %collective-permute-start.4 = (f32[32,128]{1,0:T(8,128)S(1)}, f32[32,128]{1,0:T(8,128)S(1)}, u32[]{:S(2)}, u32[]{:S(2)}) collective-permute-start(f32[32,128]{1,0:T(8,128)S(1)} %get-tuple-element.116), channel_id=1, source_target_pairs={{0,8},{1,9},{2,10},{3,11},{16,24},{17,25},{18,26},{19,27},{32,40},... | collective-permute-start | bytes 49160 | tf_op jit(solution)/shard_map/gather_diagonal/ppermute | solution.py:113
  244.2 5.8 %collective-permute-start.3 = (f32[32,128]{1,0:T(8,128)S(1)}, f32[32,128]{1,0:T(8,128)S(1)}, u32[]{:S(2)}, u32[]{:S(2)}) collective-permute-start(f32[32,128]{1,0:T(8,128)S(1)} %get-tuple-element.117), channel_id=1, source_target_pairs={{0,12},{1,13},{2,14},{3,15},{16,28},{17,29},{18,30},{19,31},{32,44... | collective-permute-start | bytes 49160 | tf_op jit(solution)/shard_map/gather_diagonal/ppermute | solution.py:113
  274.2 8.4 %collective-permute-start.6 = (f32[64,512]{1,0:T(8,128)S(1)}, f32[64,512]{1,0:T(8,128)S(1)}, u32[]{:S(2)}, u32[]{:S(2)}) collective-permute-start(f32[64,512]{1,0:T(8,128)S(1)} %bitcast.187), channel_id=1, source_target_pairs={{0,64},{16,80},{32,96},{48,112},{1,65},{17,81},{33,97},{49,113},{2... | collective-permute-start | bytes 393224 | tf_op jit(solution)/shard_map/gather_diagonal/ppermute | solution.py:113
  283.2 184.4 %all-gather.12.cloned.1.call-start = ((), (), s32[]{:S(2)}) async-start(), calls=%async_computation.2 | async-start | bytes 2359296 | tf_op jit(solution)/shard_map/gather_panel_cols/all_gather | solution.py:115
  284.6 12.1 %collective-permute-start.7 = (f32[64,1024]{1,0:T(8,128)S(1)}, f32[64,1024]{1,0:T(8,128)S(1)}, u32[]{:S(2)}, u32[]{:S(2)}) collective-permute-start(f32[64,1024]{1,0:T(8,128)S(1)} %bitcast.186), channel_id=1, source_target_pairs={{0,64},{16,80},{32,96},{48,112},{1,65},{17,81},{33,97},{49,113},{2... | collective-permute-start | bytes 786440 | tf_op jit(solution)/shard_map/gather_panel_cols/ppermute | solution.py:113
  297.4 178.8 %all-gather.8.cloned.1.call-start = ((), (), s32[]{:S(2)}) async-start(), calls=%async_computation | async-start | bytes 4456448 | tf_op jit(solution)/shard_map/gather_panel_rows/all_gather | solution.py:115
  298.7 3.1 collective-permute-start.2
  299.3 16.8 %collective-permute-start.1 = (f32[512,128]{1,0:T(8,128)S(1)}, f32[512,128]{1,0:T(8,128)S(1)}, u32[]{:S(2)}, u32[]{:S(2)}) collective-permute-start(f32[512,128]{1,0:T(8,128)S(1)} %get-tuple-element.119), channel_id=1, source_target_pairs={{0,8},{1,9},{2,10},{3,11},{16,24},{17,25},{18,26},{19,27},{32,40},... | collective-permute-start | bytes 786440 | tf_op jit(solution)/shard_map/gather_panel_rows/ppermute | solution.py:113
  300.6 15.5 %collective-permute-start = (f32[512,128]{1,0:T(8,128)S(1)}, f32[512,128]{1,0:T(8,128)S(1)}, u32[]{:S(2)}, u32[]{:S(2)}) collective-permute-start(f32[512,128]{1,0:T(8,128)S(1)} %get-tuple-element.120), channel_id=1, source_target_pairs={{0,12},{1,13},{2,14},{3,15},{16,28},{17,29},{18,30},{19,31},{32,44... | collective-permute-start | bytes 786440 | tf_op jit(solution)/shard_map/gather_panel_rows/ppermute | solution.py:113
  318.9 144.1 %copy-start.3 = (f32[512,512]{1,0:T(8,128)}, f32[512,512]{1,0:T(8,128)S(1)}, u32[]{:S(2)}) copy-start(f32[512,512]{1,0:T(8,128)S(1)} %fusion.17) | copy-start | bytes 3145732
  321.2 1.0 copy-start.4
  481.1 7.8 %slice-start = ((s8[8388608]{0:T(1024)(128)(4,1)}), s8[4194304]{0:T(1024)(128)(4,1)S(1)}, s32[]{:S(2)}) async-start(s8[8388608]{0:T(1024)(128)(4,1)} %bitcast.162), calls=%async_computation.3 | async-start | bytes 8388608
  481.1 7.6 %copy-start.5 = (f32[512,512]{1,0:T(8,128)S(1)}, f32[512,512]{1,0:T(8,128)}, u32[]{:S(2)}) copy-start(f32[512,512]{1,0:T(8,128)} %get-tuple-element.96) | copy-start | bytes 3145732
  481.2 7.8 %slice-start.1 = ((s8[8388608]{0:T(1024)(128)(4,1)}), s8[4194304]{0:T(1024)(128)(4,1)S(1)}, s32[]{:S(2)}) async-start(s8[8388608]{0:T(1024)(128)(4,1)} %bitcast.162), calls=%async_computation.4 | async-start | bytes 8388608
Sparse Core Ops, SparseCore 0:
  283.3 27.0 all-gather.9
  312.2 25.7 all-gather.11
  340.1 53.4 all-gather.7
